TPU v7x, 32 devices: a whole 2x2x4 slice. The times are simulated.
32 devices in a mesh: fsdp: 8 (over y, x, core), seq: 4 (over z).
Axes of the slice: x: 2, y: 2, z: 4, core: 2. Of those that a mesh axis runs over, the one named last changes fastest.
Arguments:
- tokens: bfloat16 [24, 584, 1024], P('fsdp', 'seq'), may hold values from -6 to 6
- counts: int32 [24], P('fsdp'), may hold values from 0 to 577, as said below
- norm1_gain: bfloat16 [1024], P('fsdp'), may hold values from 0.099609375 to 1.8984375
- norm1_shift: bfloat16 [1024], P('fsdp'), may hold values from -3 to 3
- qkv_weight: bfloat16 [1024, 3072], P('fsdp'), may hold values from -0.1875 to 0.1875
- query_bias: bfloat16 [1024], P('fsdp'), may hold values from -3 to 3
- value_bias: bfloat16 [1024], P('fsdp'), may hold values from -3 to 3
- out_weight: bfloat16 [1024, 1024], P('fsdp'), may hold values from -0.875 to 0.875
- out_bias: bfloat16 [1024], P('fsdp'), may hold values from -3 to 3
- norm2_gain: bfloat16 [1024], P('fsdp'), may hold values from 0.099609375 to 1.8984375
- norm2_shift: bfloat16 [1024], P('fsdp'), may hold values from -3 to 3
- fc1_weight: bfloat16 [1024, 4096], P('fsdp'), may hold values from -0.1875 to 0.1875
- fc1_bias: bfloat16 [4096], P('fsdp'), may hold values from -3 to 3
- fc2_weight: bfloat16 [4096, 1024], P('fsdp'), may hold values from -0.09375 to 0.09375
- fc2_bias: bfloat16 [1024], P('fsdp'), may hold values from -3 to 3
- cotangent: bfloat16 [24, 584, 1024], P('fsdp', 'seq'), may hold values from -6 to 6
Outputs:
- output: bfloat16 [24, 584, 1024], P('fsdp', 'seq')
- input_grad: float32 [24, 584, 1024], P('fsdp', 'seq')
- norm1_gain_grad: float32 [1024], P('fsdp')
- norm1_shift_grad: float32 [1024], P('fsdp')
- qkv_weight_grad: float32 [1024, 3072], P('fsdp')
- query_bias_grad: float32 [1024], P('fsdp')
- value_bias_grad: float32 [1024], P('fsdp')
- out_weight_grad: float32 [1024, 1024], P('fsdp')
- out_bias_grad: float32 [1024], P('fsdp')
- norm2_gain_grad: float32 [1024], P('fsdp')
- norm2_shift_grad: float32 [1024], P('fsdp')
- fc1_weight_grad: float32 [1024, 4096], P('fsdp')
- fc1_bias_grad: float32 [4096], P('fsdp')
- fc2_weight_grad: float32 [4096, 1024], P('fsdp')
- fc2_bias_grad: float32 [1024], P('fsdp')
Inputs may be any that keep to these rules, and one draw needn't show every extreme that they name: `counts`: each image's count is 577 or 0; image 0 has 577 and the last image has 0.
All inputs are finite; a program needn't handle non-finite values.
Results may differ from a plain program's by a relative error of at most 0.012.
Values may be sent and summed in bfloat16 or wider, within the bound.
No kernel may reach another device: no remote copies, remote signals or barrier semaphores. Data moves between devices by JAX's collectives and lax.ppermute only.
A program may use at most 192 MiB of HBM per device.

v0:
```python
import functools

import jax
import jax.numpy as jnp
from jax import lax
from jax.experimental import pallas as pl
from jax.experimental.pallas import tpu as pltpu
from jax.sharding import PartitionSpec as P

HEAD_DIM = 64
EPS = 1e-05
MASKED = -1e30
SCALE = HEAD_DIM ** (-0.5)
F32 = jnp.float32
BF16 = jnp.bfloat16
PIECES = 8
HINT = 64
COVER = 1 << 27
LONG = ("attend_back",)
LIMIT = 62 * 1024 * 1024


def call(body, grid, in_specs, out_specs, out_shape, scratch, flops, moved, name):
    return pl.pallas_call(
        body,
        grid_spec=pltpu.PrefetchScalarGridSpec(
            num_scalar_prefetch=1,
            grid=grid,
            in_specs=in_specs,
            out_specs=out_specs,
            scratch_shapes=scratch,
        ),
        out_shape=out_shape,
        compiler_params=pltpu.CompilerParams(
            dimension_semantics=("arbitrary",) * len(grid), vmem_limit_bytes=LIMIT
        ),
        cost_estimate=pl.CostEstimate(
            flops=0,
            bytes_accessed=COVER if name in LONG else moved // HINT,
            transcendentals=0,
        ),
        name=name,
    )


def whole(shape):
    return pl.BlockSpec(shape, lambda *_: (0,) * len(shape))


def dot_nn(left, right):
    return lax.dot_general(left, right, (((1,), (0,)), ((), ())), preferred_element_type=F32)


def dot_nt(left, right):
    return lax.dot_general(left, right, (((1,), (1,)), ((), ())), preferred_element_type=F32)


def dot_tn(left, right):
    return lax.dot_general(left, right, (((0,), (0,)), ((), ())), preferred_element_type=F32)


def lanes(ref, block, width):
    return ref[:, pl.ds(pl.multiple_of(block * width, 128), width)]


def put_lanes(ref, block, width, value):
    ref[:, pl.ds(pl.multiple_of(block * width, 128), width)] = value


def reorder(into, source, count, where):
    width = into.shape[1] // count

    @pl.loop(0, count)
    def _(r):
        put_lanes(into, r, width, lanes(source, where(r), width))


def stats(values):
    average = jnp.mean(values, axis=-1, keepdims=True)
    centered = values - average
    inverse = lax.rsqrt(jnp.mean(centered * centered, axis=-1, keepdims=True) + EPS)
    return centered * inverse, inverse


def stacked(refs, rows=None):
    return jnp.concatenate([r[...] if rows is None else r[:rows, :] for r in refs], axis=0)


def project_body(scal, *refs, rows, unit):
    x, gain, shift, bias_q, bias_v = refs[:5]
    weights = refs[5:13]
    out, normed, rel = refs[13:]
    step = pl.program_id(0)

    @pl.when(pl.program_id(0) == 0)
    def _():
        @pl.loop(0, rows // unit)
        def _(b):
            span = pl.ds(pl.multiple_of(b * unit, 8), unit)
            normal, _ = stats(x[span, :].astype(F32))
            normed[span, :] = (normal * gain[...] + shift[...]).astype(BF16)

        reorder(rel, normed, PIECES, lambda r: scal[0] ^ r)

    value = dot_nn(rel[...], stacked(weights, rel.shape[1] // PIECES))
    bias = jnp.where(step == 0, bias_q[...], jnp.where(step == 2, bias_v[...], 0.0))
    out[...] = (value + bias).astype(BF16)


def project(scal, x, gain, shift, bias_q, bias_v, pieces, n_seq, slot, unit):
    rows, features = x.shape
    group = features // n_seq
    depth = pieces[0].shape[0]
    return call(
        functools.partial(project_body, rows=rows, unit=unit),
        (3,),
        [whole((rows, features))]
        + [whole((1, features))] * 2
        + [pl.BlockSpec((1, group), lambda j, s: (0, s[1]))] * 2
        + [pl.BlockSpec((depth, group), lambda j, s: (0, n_seq * j + s[1]))] * PIECES,
        [pl.BlockSpec((rows, group), lambda j, s: (0, j)), whole((rows, features))],
        [
            jax.ShapeDtypeStruct((rows, 3 * group), BF16),
            jax.ShapeDtypeStruct((rows, features), BF16),
        ],
        [pltpu.VMEM((rows, features), BF16)],
        2 * rows * features * 3 * group,
        4 * rows * features + 6 * features * group,
        "project",
    )(scal, x, gain, shift, bias_q, bias_v, *pieces)


def unpack_body(scal, *refs):
    pieces, outs = refs[:PIECES], refs[PIECES:]
    for r, piece in enumerate(pieces):
        row = 0
        for out in outs:
            count = out.shape[1] // (PIECES * piece.shape[1])
            for k in range(count):
                put_lanes(
                    out,
                    (scal[0] ^ r) * count + k,
                    piece.shape[1],
                    piece[row : row + 1, :].astype(F32),
                )
                row += 1


def unpack(scal, pieces, start, sizes):
    outs = [jax.ShapeDtypeStruct((1, size), F32) for size in sizes]
    return call(
        unpack_body,
        (1,),
        [pl.BlockSpec((16, 128), lambda n, s: (start // 16, 0))] * PIECES,
        [whole(o.shape) for o in outs],
        outs,
        [],
        0,
        0,
        "unpack",
    )(scal, *pieces)


def half_masks(unit):
    lane = lax.broadcasted_iota(jnp.int32, (unit, 2 * HEAD_DIM), 1)
    return lane < HEAD_DIM


def split_heads(value, low):
    zero = jnp.zeros_like(value)
    return jnp.concatenate([jnp.where(low, value, zero), jnp.where(low, zero, value)], axis=0)


def join_heads(value, low, unit):
    return jnp.where(low, value[:unit], value[unit:])


def attend_body(scal, *refs, n_seq, unit):
    queries, keys, values = refs[:n_seq], refs[n_seq : 2 * n_seq], refs[2 * n_seq : 3 * n_seq]
    mask, out, lse = refs[3 * n_seq :]
    low = half_masks(unit)
    key = stacked(keys)
    value = stacked(values)
    for s in range(n_seq):
        scores = dot_nt(split_heads(queries[s][...], low), key) * SCALE + mask[0]
        top = jnp.max(scores, axis=-1, keepdims=True)
        weight = jnp.exp(scores - top)
        total = jnp.sum(weight, axis=-1, keepdims=True)
        probs = (weight * (1.0 / total)).astype(BF16)
        out[scal[1] ^ s] = join_heads(dot_nn(probs, value), low, unit).astype(BF16)
        log_total = top + jnp.log(total)
        lse[0, 0, s * unit : (s + 1) * unit, :] = jnp.where(
            low, log_total[:unit], log_total[unit:]
        )


def qkv_specs(n_seq, unit, pairs):
    specs = []
    for j in range(3):
        specs += [
            pl.BlockSpec((unit, 2 * HEAD_DIM), lambda b, p, s, j=j: (b, pairs * j + p))
        ] * n_seq
    return specs


def attend(scal, projected, mask, unit, images):
    n_seq = len(projected)
    rows, wide = projected[0].shape
    group = wide // 3
    pairs = group // (2 * HEAD_DIM)
    tokens = n_seq * unit
    return call(
        functools.partial(attend_body, n_seq=n_seq, unit=unit),
        (images, pairs),
        qkv_specs(n_seq, unit, pairs) + [pl.BlockSpec((1, 1, tokens), lambda b, p, s: (b, 0, 0))],
        [
            pl.BlockSpec((n_seq, unit, 2 * HEAD_DIM), lambda b, p, s: (0, b, p)),
            pl.BlockSpec((1, 1, tokens, 2 * HEAD_DIM), lambda b, p, s: (b, p, 0, 0)),
        ],
        [
            jax.ShapeDtypeStruct((n_seq, rows, group), BF16),
            jax.ShapeDtypeStruct((images, pairs, tokens, 2 * HEAD_DIM), F32),
        ],
        [],
        images * pairs * 2 * tokens * tokens * 2 * HEAD_DIM * 4,
        n_seq * rows * wide * 4,
        "attend",
    )(scal, *projected, *projected, *projected, mask)


def put_slot(ref, slot, block, value):
    width = value.shape[1]
    ref[slot, :, pl.ds(pl.multiple_of(block * width, 128), width)] = value


def attend_back_body(scal, *refs, n_seq, unit, pairs):
    queries, keys, values = refs[:n_seq], refs[n_seq : 2 * n_seq], refs[2 * n_seq : 3 * n_seq]
    grads, mask, lse, out, key_acc, value_acc, held = refs[3 * n_seq :]
    pair = pl.program_id(1)
    low = half_masks(unit)
    key = stacked(keys)
    value = stacked(values)
    for s in range(n_seq):
        held[s] = queries[s][...]
    key_acc[...] = jnp.zeros_like(key_acc)
    value_acc[...] = jnp.zeros_like(value_acc)

    def one(s):
        query = split_heads(held[s], low)
        slot = scal[1] ^ s
        grad = split_heads(grads[slot], low)
        scores = dot_nt(query, key) * SCALE + mask[0]
        saved = lse[0, 0, pl.ds(pl.multiple_of(s * unit, 8), unit), :]
        column = jnp.concatenate([saved[:, :1], saved[:, HEAD_DIM : HEAD_DIM + 1]], axis=0)
        probs = jnp.exp(scores - column)
        grad_probs = dot_nt(grad, value)
        value_part = dot_tn(probs.astype(BF16), grad)
        center = jnp.sum(grad_probs * probs, axis=-1, keepdims=True)
        grad_scores = (probs * (grad_probs - center)).astype(BF16)
        query_grad = join_heads(dot_nn(grad_scores, key), low, unit) * SCALE
        key_part = dot_tn(grad_scores, query)
        put_slot(out, slot, pair, query_grad.astype(BF16))
        return key_part, value_part

    @pl.loop(0, n_seq, step=2)
    def _(s):
        first, second = one(s), one(s + 1)
        key_acc[...] += first[0] + second[0]
        value_acc[...] += first[1] + second[1]

    for s in range(n_seq):
        span = pl.ds(s * unit, unit)
        slot = scal[1] ^ s
        put_slot(out, slot, pairs + pair, (key_acc[span, :] * SCALE).astype(BF16))
        put_slot(out, slot, 2 * pairs + pair, value_acc[span, :].astype(BF16))


def attend_back(scal, projected, grads, mask, lse, unit, images):
    n_seq = len(projected)
    rows, wide = projected[0].shape
    group = wide // 3
    pairs = group // (2 * HEAD_DIM)
    tokens = n_seq * unit
    return call(
        functools.partial(attend_back_body, n_seq=n_seq, unit=unit, pairs=pairs),
        (images, pairs),
        qkv_specs(n_seq, unit, pairs)
        + [
            pl.BlockSpec((n_seq, unit, 2 * HEAD_DIM), lambda b, p, s: (0, b, p)),
            pl.BlockSpec((1, 1, tokens), lambda b, p, s: (b, 0, 0)),
            pl.BlockSpec((1, 1, tokens, 2 * HEAD_DIM), lambda b, p, s: (b, p, 0, 0)),
        ],
        pl.BlockSpec((n_seq, unit, wide), lambda b, p, s: (0, b, 0)),
        jax.ShapeDtypeStruct((n_seq, rows, wide), BF16),
        [pltpu.VMEM((tokens, 2 * HEAD_DIM), F32)] * 2
        + [pltpu.VMEM((n_seq, unit, 2 * HEAD_DIM), BF16)],
        images * pairs * 2 * tokens * tokens * 2 * HEAD_DIM * 10,
        n_seq * rows * wide * 4,
        "attend_back",
    )(scal, *projected, *projected, *projected, grads, mask, lse)


def mix_body(scal, *refs, n_seq):
    contexts, x, bias, gain, shift = refs[:5]
    weights = refs[5:13]
    context, mixed, normed, rel = refs[13:]
    group = contexts.shape[2]

    @pl.loop(0, n_seq)
    def _(t):
        put_lanes(context, t, group, contexts[t])

    reorder(rel, context, PIECES, lambda r: scal[0] ^ r)
    branch = dot_nn(rel[...], stacked(weights)) + bias[...]
    flag = (scal[2 + pl.program_id(0)] > 0).astype(F32)
    value = x[...].astype(F32) + branch * flag
    mixed[...] = value
    normal, _ = stats(value)
    normed[...] = (normal * gain[...] + shift[...]).astype(BF16)


def mix(scal, contexts, x, bias, gain, shift, pieces, unit):
    n_seq = contexts.shape[0]
    rows, features = x.shape
    group = features // n_seq
    row_block = pl.BlockSpec((unit, features), lambda b, s: (b, 0))
    return call(
        functools.partial(mix_body, n_seq=n_seq),
        (rows // unit,),
        [pl.BlockSpec((n_seq, unit, group), lambda b, s: (0, b, 0)), row_block]
        + [whole((1, features))] * 3
        + [whole(pieces[0].shape)] * PIECES,
        [row_block] * 3,
        [
            jax.ShapeDtypeStruct((rows, features), BF16),
            jax.ShapeDtypeStruct((rows, features), F32),
            jax.ShapeDtypeStruct((rows, features), BF16),
        ],
        [pltpu.VMEM((unit, features), BF16)],
        2 * rows * features * features,
        12 * rows * features + 2 * features * features,
        "mix",
    )(scal, contexts, x, bias, gain, shift, *pieces)


def widen_body(scal, x, bias, grad, weight, active, grad_hidden):
    hidden = dot_nn(x[...], weight[...]) + bias[...]
    gate = jax.nn.sigmoid(1.702 * hidden)
    product = hidden * gate
    active[...] = product.astype(BF16)
    slope = gate + 1.702 * product * (1.0 - gate)
    grad_hidden[...] = (grad[...].astype(F32) * slope).astype(BF16)


def widen(scal, x, bias, grad, weight, tile=512):
    rows, features = x.shape
    hidden = weight.shape[1]
    column = pl.BlockSpec((rows, tile), lambda n, s: (0, n))
    return call(
        widen_body,
        (hidden // tile,),
        [
            whole((rows, features)),
            pl.BlockSpec((1, tile), lambda n, s: (0, n)),
            column,
            pl.BlockSpec((features, tile), lambda n, s: (0, n)),
        ],
        [column] * 2,
        [jax.ShapeDtypeStruct((rows, hidden), BF16)] * 2,
        [],
        2 * rows * features * hidden,
        2 * features * hidden + 6 * rows * hidden,
        "widen",
    )(scal, x, bias, grad, weight)


def narrow_body(scal, x, mixed, bias, weight, out, held, *, unit, keep):
    held[...] = dot_nn(x[...], weight[...]) + mixed[...] + bias[...]

    @pl.loop(0, out.shape[0])
    def _(b):
        span = pl.ds(pl.multiple_of(b * unit, 8), unit)
        out[b] = held[span, :][:keep].astype(BF16)


def narrow(scal, x, mixed, bias, weight, unit, keep, tile=256):
    rows, hidden = x.shape
    features = weight.shape[1]
    images = rows // unit
    column = lambda depth: pl.BlockSpec((depth, tile), lambda n, s: (0, n))
    return call(
        functools.partial(narrow_body, unit=unit, keep=keep),
        (features // tile,),
        [whole((rows, hidden)), column(rows), column(1), column(hidden)],
        pl.BlockSpec((images, keep, tile), lambda n, s: (0, 0, n)),
        jax.ShapeDtypeStruct((images, keep, features), BF16),
        [pltpu.VMEM((rows, tile), F32)],
        2 * rows * features * hidden,
        2 * features * hidden + 2 * rows * hidden + 6 * rows * features,
        "narrow",
    )(scal, x, mixed, bias, weight)


def outer_rows_body(scal, left, right, *refs):
    value = dot_tn(left[...], right[...])
    if len(refs) == 1:
        refs[0][0] = value.astype(BF16)
        return
    held = refs[-1]
    held[...] = (value + refs[0][0].astype(F32)).astype(BF16)
    part = held.shape[0] // 8
    for m, out in enumerate(refs[1:-1]):

        @pl.when(pl.program_id(0) == m)
        def _(out=out):
            @pl.loop(0, 8)
            def _(i):
                span = pl.ds(pl.multiple_of(i * part, 16), part)
                out[span, :] = held[span, :]


def outer_rows(scal, left, right, offset, added=None):
    rows, hidden = left.shape
    width = hidden // PIECES
    features = right.shape[1]
    block = pl.BlockSpec((1, width, features), lambda m, s: (m, 0, 0))
    half = PIECES // 2
    own = added is not None
    return call(
        outer_rows_body,
        (half,),
        [
            pl.BlockSpec((rows, width), lambda m, s: (0, s[0] ^ (2 * m + offset))),
            whole((rows, features)),
        ]
        + ([block] if own else []),
        [whole((width, features))] * half if own else block,
        [jax.ShapeDtypeStruct((width, features), BF16)] * half
        if own
        else jax.ShapeDtypeStruct((half, width, features), BF16),
        [pltpu.VMEM((width, features), BF16)] if own else [],
        rows * hidden * features,
        hidden * features * (2 if own else 1),
        f"outer_rows{offset}",
    )(scal, left, right, *((added,) if own else ()))


def outer_body(scal, *refs, count, offset, width):
    lefts, right = refs[:count], refs[count]
    rel, acc = refs[-2:]
    half = PIECES // 2

    @pl.when(pl.program_id(0) == 0)
    def _():
        for i in range(count):
            reorder(rel.at[i], lefts[i], half, lambda m: scal[0] ^ (2 * m + offset))

    acc[...] = jnp.zeros_like(acc)

    @pl.loop(0, count)
    def _(i):
        acc[...] += dot_tn(rel[i], right[scal[1] ^ i])

    for m in range(half):
        part = acc[m * width : (m + 1) * width, :]
        if offset == 0:
            outs = refs[count + 2 : -2]
            outs[m][...] = (part + refs[count + 1][m].astype(F32)).astype(BF16)
        else:
            refs[count + 1][m] = part.astype(BF16)
    if offset:
        refs[count + 2][...] = sum(rows_sum(right[i].astype(F32)) for i in range(count))


def outer(scal, lefts, right, offset, tile, added=None, name=""):
    count = len(lefts)
    rows, features = lefts[0].shape
    wide = right.shape[2]
    width = features // PIECES
    half = PIECES // 2
    block = pl.BlockSpec((half, width, tile), lambda n, s: (0, 0, n))
    own = added is not None
    return call(
        functools.partial(outer_body, count=count, offset=offset, width=width),
        (wide // tile,),
        [whole((rows, features))] * count
        + [pl.BlockSpec((count, rows, tile), lambda n, s: (0, 0, n))]
        + ([block] if own else []),
        [pl.BlockSpec((width, tile), lambda n, s: (0, n))] * half
        if own
        else [block, pl.BlockSpec((1, tile), lambda n, s: (0, n))],
        [jax.ShapeDtypeStruct((width, wide), BF16)] * half
        if own
        else [
            jax.ShapeDtypeStruct((half, width, wide), BF16),
            jax.ShapeDtypeStruct((1, wide), F32),
        ],
        [
            pltpu.VMEM((count, rows, half * width), BF16),
            pltpu.VMEM((half * width, tile), F32),
        ],
        count * rows * features * wide,
        features * wide * (1 if offset else 2) + count * 2 * rows * (features + wide),
        f"outer_{name}{offset}",
    )(scal, *lefts, right, *(() if added is None else (added,)))


def outer_two_body(scal, *refs, offset, width, first):
    lefts, rights = refs[:2], refs[2:4]
    rels = refs[-2:]
    half = PIECES // 2
    step = pl.program_id(0)

    @pl.when(step == 0)
    def _():
        for left, rel in zip(lefts, rels):
            reorder(rel, left, half, lambda m: scal[0] ^ (2 * m + offset))

    def store(value):
        for m in range(half):
            part = value[m * width : (m + 1) * width]
            if offset == 0:
                refs[5 + m][...] = (part + refs[4][m].astype(F32)).astype(BF16)
            else:
                refs[4][m] = part.astype(BF16)

    @pl.when(step < first)
    def _():
        store(dot_tn(rels[0][...], rights[0][...]))

    @pl.when(step >= first)
    def _():
        store(dot_tn(rels[1][...], rights[1][...]))


def outer_two(scal, lefts, rights, offset, added=None, tile=512):
    rows, features = lefts[0].shape
    first = rights[0].shape[1] // tile
    count = first + rights[1].shape[1] // tile
    wide = count * tile
    width = features // PIECES
    half = PIECES // 2
    block = pl.BlockSpec((half, width, tile), lambda n, s: (0, 0, n))
    own = added is not None
    return call(
        functools.partial(outer_two_body, offset=offset, width=width, first=first),
        (count,),
        [whole((rows, features))] * 2
        + [
            pl.BlockSpec((rows, tile), lambda n, s: (0, jnp.minimum(n, first - 1))),
            pl.BlockSpec((rows, tile), lambda n, s: (0, jnp.maximum(n - first, 0))),
        ]
        + ([block] if own else []),
        [pl.BlockSpec((width, tile), lambda n, s: (0, n))] * half if own else block,
        [jax.ShapeDtypeStruct((width, wide), BF16)] * half
        if own
        else jax.ShapeDtypeStruct((half, width, wide), BF16),
        [pltpu.VMEM((rows, half * width), BF16)] * 2,
        rows * features * wide,
        features * wide * (2 if own else 1),
        f"outer_two{offset}",
    )(scal, *lefts, *rights, *((added,) if own else ()))


def narrow_back_body(scal, grad, weight, out):
    out[...] = dot_nt(grad[...], weight[...]).astype(BF16)


def narrow_back(scal, grad, weight, tile=512):
    rows, features = grad.shape
    hidden = weight.shape[0]
    return call(
        narrow_back_body,
        (hidden // tile,),
        [whole((rows, features)), pl.BlockSpec((tile, features), lambda n, s: (n, 0))],
        pl.BlockSpec((rows, tile), lambda n, s: (0, n)),
        jax.ShapeDtypeStruct((rows, hidden), BF16),
        [],
        2 * rows * features * hidden,
        2 * features * hidden + 2 * rows * hidden,
        "narrow_back",
    )(scal, grad, weight)


def norm_back(grad, normal, inverse, gain):
    scaled = grad * gain
    return inverse * (
        scaled
        - jnp.mean(scaled, axis=-1, keepdims=True)
        - normal * jnp.mean(scaled * normal, axis=-1, keepdims=True)
    )


def clear(ref, unit, condition):
    @pl.when(condition)
    def _():
        @pl.loop(0, ref.shape[0] // unit)
        def _(b):
            span = pl.ds(pl.multiple_of(b * unit, 8), unit)
            ref[span, :] = jnp.zeros((unit, ref.shape[1]), ref.dtype)


def rows_sum(value):
    return jnp.sum(value, axis=0, keepdims=True)


def widen_back_body(scal, *refs, unit):
    grad, mixed, dy, gain, weight = refs[:5]
    dmixed, dbranch, sums, bias_sum, acc = refs[5:]
    step = pl.program_id(0)
    value = grad[...]
    bias_sum[...] = rows_sum(value.astype(F32))
    clear(acc, unit, step == 0)
    part = dot_nt(value, weight[...])

    acc[...] += part

    @pl.when(step == pl.num_programs(0) - 1)
    def _():
        def image(b, totals):
            span = pl.ds(pl.multiple_of(b * unit, 8), unit)
            normal, inverse = stats(mixed[span, :])
            grad_out = dy[span, :].astype(F32)
            back = acc[span, :]
            total = grad_out + norm_back(back, normal, inverse, gain[...])
            dmixed[span, :] = total
            flag = (scal[2 + b] > 0).astype(F32)
            low = (total * flag).astype(BF16)
            dbranch[span, :] = low
            parts = (back * normal, back, low.astype(F32), grad_out)
            return tuple(t + rows_sum(p) for t, p in zip(totals, parts))

        none = jnp.zeros((1, acc.shape[1]), F32)
        totals = lax.fori_loop(0, acc.shape[0] // unit, image, (none,) * 4)
        sums[...] = jnp.concatenate(list(totals) + [none] * 4, axis=0)


def widen_back(scal, grad, mixed, dy, gain, weight, unit, tile=1024):
    rows, hidden = grad.shape
    features = mixed.shape[1]
    full = whole((rows, features))
    return call(
        functools.partial(widen_back_body, unit=unit),
        (hidden // tile,),
        [
            pl.BlockSpec((rows, tile), lambda n, s: (0, n)),
            full,
            full,
            whole((1, features)),
            pl.BlockSpec((features, tile), lambda n, s: (0, n)),
        ],
        [
            full,
            full,
            whole((8, features)),
            pl.BlockSpec((1, tile), lambda n, s: (0, n)),
        ],
        [
            jax.ShapeDtypeStruct((rows, features), F32),
            jax.ShapeDtypeStruct((rows, features), BF16),
            jax.ShapeDtypeStruct((8, features), F32),
            jax.ShapeDtypeStruct((1, hidden), F32),
        ],
        [pltpu.VMEM((rows, features), F32)],
        2 * rows * features * hidden,
        2 * features * hidden + 2 * rows * hidden + 12 * rows * features,
        "widen_back",
    )(scal, grad, mixed, dy, gain, weight)


def mix_back_body(scal, *refs, n_seq):
    grad = refs[0]
    weights = refs[1:9]
    out, rel = refs[9:]
    rel[...] = dot_nt(grad[...], stacked(weights)).astype(BF16)
    width = rel.shape[1] // PIECES
    per = PIECES // n_seq

    @pl.loop(0, n_seq)
    def _(t):
        for k in range(per):
            out[t, :, k * width : (k + 1) * width] = lanes(
                rel, scal[0] ^ (t * per + k), width
            )


def mix_back(scal, grad, pieces, n_seq, unit):
    rows, features = grad.shape
    group = features // n_seq
    return call(
        functools.partial(mix_back_body, n_seq=n_seq),
        (rows // unit,),
        [pl.BlockSpec((unit, features), lambda b, s: (b, 0))] + [whole(pieces[0].shape)] * PIECES,
        pl.BlockSpec((n_seq, unit, group), lambda b, s: (0, b, 0)),
        jax.ShapeDtypeStruct((n_seq, rows, group), BF16),
        [pltpu.VMEM((unit, features), BF16)],
        2 * rows * features * features,
        4 * rows * features + 2 * features * features,
        "mix_back",
    )(scal, grad, *pieces)


def project_back_body(scal, *refs, n_seq, unit, keep):
    grads, x, dmixed, gain = refs[:4]
    weights = refs[4:12]
    out, sums, acc, nat, wide = refs[12:]
    step = pl.program_id(0)
    width = acc.shape[1] // PIECES
    @pl.loop(0, n_seq)
    def _(t):
        put_lanes(wide, t, grads.shape[2], grads[t])

    clear(acc, unit, step == 0)
    part = dot_nt(wide[...], stacked(weights, width))

    acc[...] += part

    @pl.when(step == pl.num_programs(0) - 1)
    def _():
        def image(b, totals):
            span = pl.ds(pl.multiple_of(b * unit, 8), unit)

            @pl.loop(0, PIECES)
            def _(r):
                part = acc[span, pl.ds(pl.multiple_of(r * width, 128), width)]
                put_lanes(nat, scal[0] ^ r, width, part)

            normal, inverse = stats(x[span, :].astype(F32))
            back = nat[...]
            total = dmixed[span, :] + norm_back(back, normal, inverse, gain[...])
            out[b] = total[:keep]
            return tuple(t + rows_sum(p) for t, p in zip(totals, (back * normal, back)))

        none = jnp.zeros((1, acc.shape[1]), F32)
        totals = lax.fori_loop(0, acc.shape[0] // unit, image, (none,) * 2)
        sums[...] = jnp.concatenate(list(totals) + [none] * 6, axis=0)


def project_back(scal, grads, x, dmixed, gain, pieces, unit, keep):
    n_seq = grads.shape[0]
    rows, features = x.shape
    group = features // n_seq
    depth = pieces[0].shape[0]
    images = rows // unit
    full = whole((rows, features))
    return call(
        functools.partial(project_back_body, n_seq=n_seq, unit=unit, keep=keep),
        (3,),
        [
            pl.BlockSpec((n_seq, rows, group), lambda j, s: (0, 0, j)),
            full,
            full,
            whole((1, features)),
        ]
        + [pl.BlockSpec((depth, features), lambda j, s: (0, j))] * PIECES,
        [whole((images, keep, features)), whole((8, features))],
        [
            jax.ShapeDtypeStruct((images, keep, features), F32),
            jax.ShapeDtypeStruct((8, features), F32),
        ],
        [
            pltpu.VMEM((rows, features), F32),
            pltpu.VMEM((unit, features), F32),
            pltpu.VMEM((rows, features), BF16),
        ],
        6 * rows * features * features,
        6 * features * features + 16 * rows * features,
        "project_back",
    )(scal, grads, x, dmixed, gain, *pieces)


def flip(value, bit):
    return lax.ppermute(value, "fsdp", [(i, i ^ bit) for i in range(PIECES)])


def flip_mixed(value):
    return lax.ppermute(
        value, "fsdp", [(i, i ^ (4 if i & 1 else 2)) for i in range(PIECES)]
    )


def after(value, *others):
    return lax.optimization_barrier((value, others))[0]


def spread_near(shard):
    return flip(shard, 2), flip(shard, 4), flip(shard, 1)


def spread_far(near, odd, gate=()):
    return flip_mixed(after(jnp.where(odd, near[0], near[1]), gate))


def spread_rest(shard, near, far, near_gate=(), far_gate=()):
    return [
        shard,
        near[2],
        near[0],
        flip(after(near[0], near_gate), 1),
        near[1],
        flip(after(near[1], near_gate), 1),
        far,
        flip(after(far, far_gate), 1),
    ]


def gather_whole(shard):
    full = lax.all_gather(shard, "fsdp", axis=0, tiled=True)
    size = full.shape[0] // PIECES
    return [full[r * size : (r + 1) * size] for r in range(PIECES)]


def sides_body(scal, right, down, passed, to_x, to_y):
    odd = (scal[0] & 1) == 1
    extra = passed[...].astype(F32)
    none = jnp.zeros_like(extra)
    to_x[...] = (right[...].astype(F32) + jnp.where(odd, extra, none)).astype(BF16)
    to_y[...] = (down[...].astype(F32) + jnp.where(odd, none, extra)).astype(BF16)


def small_call(scal, body, operands, outs, name, steps=1):
    spec = lambda v: pl.BlockSpec((v.shape[0] // steps, v.shape[1]), lambda n, s: (n, 0))
    return call(
        body,
        (steps,),
        [spec(v) for v in operands],
        [spec(o) for o in outs],
        outs,
        [],
        0,
        sum(v.size for v in operands),
        name,
    )(scal, *operands)


def row_steps(value):
    return 4 if value.shape[0] % 64 == 0 else 1


def sides(scal, summed, passed):
    like = jax.ShapeDtypeStruct(passed.shape, BF16)
    return small_call(
        scal,
        sides_body,
        (summed[1], summed[2], passed),
        [like] * 2,
        "sides",
        row_steps(passed),
    )


def move_sides(pair):
    return flip(pair[0], 2), flip(pair[1], 4)


def total_body(scal, *refs):
    total = refs[0][...].astype(F32)
    for value in refs[1:-1]:
        total += value[...].astype(F32)
    refs[-1][...] = total.astype(BF16)


def total(scal, parts, half=None):
    rows, wide = parts[0].shape
    rows = rows if half is None else rows // 2
    steps = max(1, min(4, rows // 32)) if rows % 32 == 0 else 1
    block = (rows // steps, wide)
    specs = [
        pl.BlockSpec(
            block, lambda n, s, at=half * steps if p.shape[0] > rows else 0: (n + at, 0)
        )
        for p in parts
    ]
    return call(
        total_body,
        (steps,),
        specs,
        pl.BlockSpec(block, lambda n, s: (n, 0)),
        jax.ShapeDtypeStruct((rows, wide), BF16),
        [],
        0,
        0,
        "total",
    )(scal, *parts)


def copies_body(scal, *refs):
    out, small = refs[-1], refs[-2][...]
    rows = refs[0].shape[0]
    lane = small.shape[1]
    total = refs[0][...].astype(F32)
    for value in refs[1:-2]:
        total += value[...].astype(F32)
    high = small.astype(BF16)
    rest = (small - high.astype(F32)).astype(BF16)
    for t in range(out.shape[0]):
        out[t, :rows, :] = total.astype(BF16)
        out[t, rows:, :] = jnp.zeros((small.shape[0], total.shape[1]), BF16)
        out[t, rows:, :lane] = high
        out[t, rows:, lane : 2 * lane] = rest


def copies(scal, parts, small, n_seq):
    rows, wide = parts[0].shape
    shape = (n_seq, rows + small.shape[0], wide)
    return call(
        copies_body,
        (1,),
        [whole(v.shape) for v in (*parts, small)],
        whole(shape),
        jax.ShapeDtypeStruct(shape, BF16),
        [],
        0,
        0,
        "copies",
    )(scal, *parts, small)


def choose_body(scal, *refs, n_seq, count):
    inner = (scal[1] > 0) & (scal[1] < n_seq - 1)
    for k in range(count):

        @pl.when(pl.program_id(0) == k)
        def _(k=k):
            own, other = refs[k][...].astype(F32), refs[count + k][...].astype(F32)
            value = jnp.where(inner, own, other)
            at = 0
            for out in refs[2 * count :]:
                out[...] = value[:, at : at + out.shape[1]]
                at += out.shape[1]


def choose(scal, owns, others, n_seq, widths):
    count = len(owns)
    rows = owns[0].shape[0]
    return call(
        functools.partial(choose_body, n_seq=n_seq, count=count),
        (count,),
        [whole(v.shape) for v in (*owns, *others)],
        [pl.BlockSpec((rows, w), lambda n, s: (n, 0)) for w in widths],
        [jax.ShapeDtypeStruct((rows * count, w), F32) for w in widths],
        [],
        0,
        0,
        "choose",
    )(scal, *owns, *others)


def inward(value, n_seq):
    last = n_seq - 1
    return lax.ppermute(value, "seq", [(0, 1), (last, last - 1)])


def across(value):
    return lax.ppermute(value, "seq", [(1, 2), (2, 1)])


def outward(value, n_seq):
    last = n_seq - 1
    return lax.ppermute(value, "seq", [(1, 0), (last - 1, last)])


def join_body(scal, parts, out, small):
    count = parts.shape[0]
    width = parts.shape[2] // 3
    rows, lane = out.shape[0], small.shape[1]
    total = 0.0
    for t in range(count):
        for j in range(3):
            at = (j * count + t) * width
            out[:, at : at + width] = parts[t, :rows, j * width : (j + 1) * width].astype(F32)
        for j in range(2):
            total += parts[t, rows:, j * lane : (j + 1) * lane].astype(F32)
    small[...] = total


def join(scal, parts, rows, lane):
    count, tall, wide = parts.shape
    shapes = (rows, wide * count), (tall - rows, lane)
    return call(
        join_body,
        (1,),
        [whole(parts.shape)],
        [whole(v) for v in shapes],
        [jax.ShapeDtypeStruct(v, F32) for v in shapes],
        [],
        0,
        0,
        "join",
    )(scal, parts)


def scatter_whole(theirs, mine):
    full = jnp.stack([jnp.stack(mine), theirs], axis=1)
    full = full.reshape(PIECES * full.shape[2], full.shape[3])
    return lax.psum_scatter(full.astype(F32), "fsdp", scatter_dimension=0, tiled=True)


def swap_seq(value, bits, n_seq):
    if bits == 0:
        return value
    return lax.ppermute(value, "seq", [(i, i ^ bits) for i in range(n_seq)])


def hop(pair, t, n_seq):
    up = lax.ppermute(pair[0], "seq", [(i, i + 1) for i in range(t - 1, n_seq - 1)])
    down = lax.ppermute(pair[1], "seq", [(i + 1, i) for i in range(0, n_seq - t)])
    return up, down


def pick(hops, s, place, n_seq, gate):
    used = sorted({abs((p ^ s) - p) for p in range(n_seq)})
    hops = dict(zip(used, after([hops[d - 1] for d in used], gate)))
    value = None
    for p in range(n_seq):
        distance = (p ^ s) - p
        case = hops[abs(distance)][1 if distance > 0 else 0]
        value = case if value is None else jnp.where(place == p, case, value)
    return value


def exchange(value):
    return lax.all_to_all(value, "seq", 0, 0, tiled=True)


def on_device(
    n_fsdp,
    n_seq,
    tokens,
    counts,
    norm1_gain,
    norm1_shift,
    qkv_weight,
    query_bias,
    value_bias,
    out_weight,
    out_bias,
    norm2_gain,
    norm2_shift,
    fc1_weight,
    fc1_bias,
    fc2_weight,
    fc2_bias,
    cotangent,
):
    images, local_len, features = tokens.shape
    unit = -(-local_len // 8) * 8
    group = features // n_seq
    shard = lax.axis_index("fsdp")
    place = lax.axis_index("seq")
    cross = n_fsdp == PIECES
    odd = (shard & 1) == 1
    me = shard if cross else jnp.zeros_like(shard)
    scal = jnp.concatenate([jnp.stack([me, place]).astype(jnp.int32), counts])
    send = lambda arrays: [swap_seq(a, t, n_seq) for t, a in enumerate(arrays)]

    def flat(v):
        v = jnp.pad(v, ((0, 0), (0, unit - local_len), (0, 0)))
        return v.reshape(images * unit, features)

    vectors = (
        norm1_gain,
        norm1_shift,
        query_bias,
        value_bias,
        out_bias,
        norm2_gain,
        norm2_shift,
        fc2_bias,
        fc1_bias,
    )

    gather = lambda v: lax.all_gather(v, "fsdp", axis=0, tiled=True)
    hops = [hop((tokens, tokens), 1, n_seq)]
    for t in range(2, n_seq):
        hops.append(hop(hops[-1], t, n_seq))
    lane = vectors[0].shape[0]
    packed = jnp.concatenate([v.reshape(-1, lane) for v in vectors], axis=0)
    if cross:
        count = packed.shape[0]
        extra = jnp.pad(packed, ((0, -count % 16), (0, qkv_weight.shape[1] - lane)))
        qkv_shard = jnp.concatenate([qkv_weight, extra], axis=0)
        near_q = (flip(qkv_shard, 2), flip(qkv_shard, 4))
        far_q = spread_far(near_q, odd, hops[0])
        near_q = (*near_q, flip(after(qkv_shard, near_q), 1))
        qkv_pieces = spread_rest(
            qkv_shard, near_q, far_q, hops[1], hops[1]
        )
        fc2_full = gather(after(fc2_weight, near_q[:2], hops[0]))
        full = unpack(
            scal, qkv_pieces, qkv_weight.shape[0], [v.shape[0] * PIECES for v in vectors]
        )
    else:
        qkv_pieces = gather_whole(qkv_weight)
        out_pieces = gather_whole(out_weight)
        fc2_full = gather(fc2_weight)
        held = lax.all_gather(packed, "fsdp", axis=0).astype(F32)
        full, at = [], 0
        for v in vectors:
            size = v.shape[0] // lane
            full.append(held[:, at : at + size].reshape(1, -1))
            at += size
    fc1_full = gather(fc1_weight)
    gain1, shift1, bias_q, bias_v, bias_o, gain2, shift2, bias_2, bias_1 = full

    spot = jnp.arange(n_seq * unit)
    inside = spot % unit
    position = ((spot // unit) ^ place) * local_len + inside
    mask = jnp.where(position[None] < counts[:, None], 0.0, MASKED)
    mask = jnp.where(inside[None] < local_len, mask, 2 * MASKED).astype(F32)[:, None]

    x = flat(tokens)
    dy = flat(cotangent)
    projected, normed = [], []
    for s in range(n_seq):
        entry = flat(pick(hops, s, place, n_seq, projected[: s - 1])) if s else x
        entry = after(entry, projected[-1:], hops[1])
        out, h = project(
            scal, entry, gain1, shift1, bias_q, bias_v, qkv_pieces, n_seq, s, unit
        )
        projected.append(out)
        normed.append(h)
    contexts, lse = attend(scal, projected, mask, unit, images)
    ready = ()
    if cross:
        near_o = spread_near(after(out_weight, projected[2]))
        far_o = spread_far(near_o, odd, lse)
        ready = near_o
    contexts = exchange(after(contexts, ready))
    grad_active = narrow_back(scal, after(dy, lse, ready), fc2_full)
    if cross:
        out_pieces = spread_rest(out_weight, near_o, far_o, lse, grad_active)
    context, mixed, normed_two = mix(
        scal,
        contexts,
        after(x, grad_active),
        bias_o,
        gain2,
        shift2,
        out_pieces,
        unit,
    )
    active, grad_hidden = widen(scal, normed_two, bias_1, grad_active, fc1_full)

    swap = (lambda v: flip(v, 1)) if cross else jnp.zeros_like
    theirs_2 = outer_rows(scal, active, dy, 1)
    other_2 = swap(theirs_2)
    dmixed, dbranch, sums2, fc1_bias_sum = widen_back(
        scal, after(grad_hidden, theirs_2), mixed, dy, gain2, fc1_full, unit
    )
    pair_left = (normed_two, context)
    pair_right = (grad_hidden, dbranch)
    theirs_1 = outer_two(scal, after(pair_left, dmixed, other_2), pair_right, 1)
    other_1 = swap(theirs_1)
    grads = mix_back(scal, after(dbranch, theirs_1), out_pieces, n_seq, unit)
    arrived = exchange(grads)
    mine_2 = outer_rows(scal, after(active, grads), dy, 0, other_2)
    passed_2 = flip_mixed(mine_2[3]) if cross else mine_2[3]
    mine_1 = outer_two(scal, after(pair_left, mine_2), pair_right, 0, other_1)
    passed_1 = flip_mixed(mine_1[3]) if cross else mine_1[3]
    back = attend_back(
        scal, projected, after(arrived, mine_1), mask, lse, unit, images
    )
    if cross:
        pair_2 = sides(scal, mine_2, after(passed_2, back))
        fc2_terms = (mine_2[0], *move_sides(pair_2))
    else:
        pair_2 = ()
        fc2_terms = (scatter_whole(theirs_2, mine_2),)
    returned = exchange(after(back, pair_2, passed_1))
    theirs_q, heads_sum = outer(
        scal, normed, after(back, pair_2), 1, group, None, "qkv"
    )
    other_q = swap(theirs_q)
    if cross:
        pair_1 = sides(scal, mine_1, after(passed_1, theirs_q))
        fc1_terms = (mine_1[0], *move_sides(pair_1))
    else:
        pair_1 = ()
        fc1_terms = (scatter_whole(theirs_1, mine_1),)
    output = narrow(
        scal,
        after(active, pair_1, theirs_q),
        mixed,
        bias_2,
        fc2_full,
        unit,
        local_len,
    )
    fc2_own = total(scal, after(fc2_terms, output, other_q))
    fc2_in = inward(fc2_own, n_seq)
    mine_q = outer(
        scal, after(normed, fc2_own), back, 0, group, other_q, "qkv"
    )
    passed_q = flip_mixed(mine_q[3]) if cross else mine_q[3]
    halves = range(2)
    fc1_terms = after(fc1_terms, mine_q)
    fc1_own = [total(scal, fc1_terms, k) for k in halves]
    fc1_in = [inward(v, n_seq) for v in fc1_own]
    input_grad, sums1 = project_back(
        scal,
        returned,
        x,
        after(dmixed, fc1_own),
        gain1,
        qkv_pieces,
        unit,
        local_len,
    )

    if cross:
        pair_q = sides(scal, mine_q, after(passed_q, input_grad))
        qkv_terms = (mine_q[0], *move_sides(pair_q))
    else:
        pair_q = ()
        qkv_terms = (scatter_whole(theirs_q, mine_q),)
    fc2_pair = total(
        scal, (*fc2_terms, after(fc2_in, input_grad, fc1_in[0], pair_q))
    )
    fc2_across = across(fc2_pair)
    fc1_pair = [total(scal, (*fc1_terms, after(fc1_in[0], fc2_pair)), 0)]
    fc1_pair += [total(scal, (*fc1_terms, after(fc1_in[1], fc1_pair)), 1)]
    fc1_across = [across(v) for v in fc1_pair]
    heads_sum = heads_sum.reshape(3, group)
    spread = lambda v: lax.dynamic_update_slice_in_dim(
        jnp.zeros((features,), F32), v, place * group, axis=0
    )
    sums = (
        sums1[0],
        sums1[1],
        spread(heads_sum[0]),
        spread(heads_sum[2]),
        sums2[2],
        sums2[0],
        sums2[1],
        sums2[3],
        fc1_bias_sum[0],
    )
    small = jnp.concatenate([v.reshape(n_fsdp, -1, lane) for v in sums], axis=1)
    if cross:
        for bit in (1, 2, 4):
            small = small + flip(small, bit)
        small = lax.dynamic_index_in_dim(small, shard, 0, False)
    else:
        small = jnp.sum(lax.all_to_all(small, "fsdp", 0, 0, tiled=True), axis=0)
    small = jnp.pad(small, ((0, -small.shape[0] % 16), (0, 0)))
    low = copies(scal, after(qkv_terms, fc1_pair), small, n_seq)
    shared = exchange(low)
    fc2_done = total(scal, (fc2_pair, after(fc2_across, low)))
    fc2_out = outward(fc2_done, n_seq)
    fc1_done = [total(scal, (fc1_pair[0], after(fc1_across[0], fc2_done)))]
    (fc2_weight_grad,) = choose(
        scal, (fc2_done,), (after(fc2_out, fc1_done),), n_seq, (features,)
    )
    fc1_done += [total(scal, (fc1_pair[1], after(fc1_across[1], fc2_weight_grad)))]
    fc1_out = [outward(v, n_seq) for v in fc1_done]
    qkv_weight_grad, small = join(
        scal, after(shared, fc1_done), qkv_weight.shape[0], lane
    )
    fc1_weight_grad, out_weight_grad = choose(
        scal,
        fc1_done,
        after(fc1_out, qkv_weight_grad),
        n_seq,
        (fc1_weight.shape[1], features),
    )
    shares, at = [], 0
    for v in vectors:
        size = v.shape[0] // lane
        shares.append(small[at : at + size].reshape(-1))
        at += size
    g1, s1, qb, vb, ob, g2, s2, b2, b1 = shares
    return (
        output,
        input_grad,
        g1,
        s1,
        qkv_weight_grad,
        qb,
        vb,
        out_weight_grad,
        ob,
        g2,
        s2,
        fc1_weight_grad,
        b1,
        fc2_weight_grad,
        b2,
    )


def solution(mesh):
    rows, vector, matrix = P("fsdp", "seq", None), P("fsdp"), P("fsdp", None)
    return jax.shard_map(
        functools.partial(on_device, mesh.shape["fsdp"], mesh.shape["seq"]),
        mesh=mesh,
        in_specs=(
            rows,
            vector,
            vector,
            vector,
            matrix,
            vector,
            vector,
            matrix,
            vector,
            vector,
            vector,
            matrix,
            vector,
            matrix,
            vector,
            rows,
        ),
        out_specs=(
            rows,
            rows,
            vector,
            vector,
            matrix,
            vector,
            vector,
            matrix,
            vector,
            vector,
            vector,
            matrix,
            vector,
            matrix,
            vector,
        ),
        check_vma=False,
    )
```

profile of v0, /device:TPU:0, one launch (start us, length us, event | category | flops | bytes accessed | tf_op | source)
XLA Modules:
  0.0 478.5 jit_solution(6859015160238107209)
XLA Ops:
  8.5 6.5 %collective-permute-start = (bf16[3,146,1024]{2,1,0:T(8,128)(2,1)}, bf16[3,146,1024]{2,1,0:T(8,128)(2,1)}, u32[]{:S(2)}, u32[]{:S(2)}) collective-permute-start(bf16[3,146,1024]{2,1,0:T(8,128)(2,1)} %param.16), channel_id=1, source_target_pairs={{0,1},{1,2},{2,3},{4,5},{5,6},{6,7},{8,9},{9,10},{10,11},{12,13},{... | collective-permute-start | bytes 2691080 | tf_op jit(solution)/shard_map/ppermute | solution.py:1006
  21.3 17.7 %collective-permute-done.5.refs_4_.refs_9_.refs_8_ = bf16[144,3072]{1,0:T(8,128)(2,1)S(1)} collective-permute-done((bf16[144,3072]{1,0:T(8,128)(2,1)S(1)}, bf16[144,3072]{1,0:T(8,128)(2,1)S(1)}, u32[]{:S(2)}, u32[]{:S(2)}) %collective-permute-start.5) | collective-permute-done | bytes 884768 | tf_op jit(solution)/shard_map/ppermute | solution.py:773
  45.7 22.9 %collective-permute-done.9.refs_6_.refs_11_.refs_10_ = bf16[144,3072]{1,0:T(8,128)(2,1)} collective-permute-done((bf16[144,3072]{1,0:T(8,128)(2,1)S(1)}, bf16[144,3072]{1,0:T(8,128)(2,1)}, u32[]{:S(2)}, u32[]{:S(2)}) %collective-permute-start.9) | collective-permute-done | bytes 884768 | tf_op jit(solution)/shard_map/ppermute | solution.py:777
  77.8 6.3 %project.4 = (bf16[456,768]{1,0:T(8,128)(2,1)}, bf16[456,1024]{1,0:T(8,128)(2,1)}) custom-call(s32[5]{0:T(128)} %pad_add_fusion.scal, bf16[456,1024]{1,0:T(8,128)(2,1)} %bitcast.69, f32[1,1024]{1,0:T(1,128)} %get-tuple-element.139.refs_1_.refs_3_, f32[1,1024]{1,0:T(1,128)} %get-tuple-element.140.refs_2_, f32[1,1024]{1,0:T(1,128)} %get-tuple-element.141.refs_3_, ...), custom_call_target="tpu_custom_call" | custom-call | bytes 53760 | tf_op jit(solution)/shard_map/project/pallas_call | solution.py:114
  88.4 6.4 %project.5 = (bf16[456,768]{1,0:T(8,128)(2,1)}, bf16[456,1024]{1,0:T(8,128)(2,1)}) custom-call(s32[5]{0:T(128)} %pad_add_fusion.scal, bf16[456,1024]{1,0:T(8,128)(2,1)} %bitcast.74, f32[1,1024]{1,0:T(1,128)} %get-tuple-element.139.refs_1_.refs_3_, f32[1,1024]{1,0:T(1,128)} %get-tuple-element.140.refs_2_, f32[1,1024]{1,0:T(1,128)} %get-tuple-element.141.refs_3_, ...), custom_call_target="tpu_custom_call" | custom-call | bytes 53760 | tf_op jit(solution)/shard_map/project/pallas_call | solution.py:114
  94.7 6.4 %project.6 = (bf16[456,768]{1,0:T(8,128)(2,1)}, bf16[456,1024]{1,0:T(8,128)(2,1)}) custom-call(s32[5]{0:T(128)} %pad_add_fusion.scal, bf16[456,1024]{1,0:T(8,128)(2,1)} %bitcast.72, f32[1,1024]{1,0:T(1,128)} %get-tuple-element.139.refs_1_.refs_3_, f32[1,1024]{1,0:T(1,128)} %get-tuple-element.140.refs_2_, f32[1,1024]{1,0:T(1,128)} %get-tuple-element.141.refs_3_, ...), custom_call_target="tpu_custom_call" | custom-call | bytes 53760 | tf_op jit(solution)/shard_map/project/pallas_call | solution.py:114
  106.0 6.5 %project.7 = (bf16[456,768]{1,0:T(8,128)(2,1)}, bf16[456,1024]{1,0:T(8,128)(2,1)}) custom-call(s32[5]{0:T(128)} %pad_add_fusion.scal, bf16[456,1024]{1,0:T(8,128)(2,1)} %bitcast.73, f32[1,1024]{1,0:T(1,128)} %get-tuple-element.139.refs_1_.refs_3_, f32[1,1024]{1,0:T(1,128)} %get-tuple-element.140.refs_2_, f32[1,1024]{1,0:T(1,128)} %get-tuple-element.141.refs_3_, ...), custom_call_target="tpu_custom_call" | custom-call | bytes 53760 | tf_op jit(solution)/shard_map/project/pallas_call | solution.py:114
  112.5 13.5 %attend.1 = (bf16[4,456,256]{2,1,0:T(8,128)(2,1)}, f32[3,2,608,128]{3,2,1,0:T(8,128)}) custom-call(s32[5]{0:T(128)} %pad_add_fusion.scal, bf16[456,768]{1,0:T(8,128)(2,1)} %get-tuple-element.143.refs_0_.refs_4_.refs_8_, bf16[456,768]{1,0:T(8,128)(2,1)} %get-tuple-element.147.refs_1_.refs_5_.refs_9_, ...), custom_call_target="tpu_custom_call" | custom-call | bytes 87552 | tf_op jit(solution)/shard_map/attend/pallas_call | solution.py:212
  126.0 6.4 %all-to-all-start = ((bf16[4,456,256]{2,1,0:T(8,128)(2,1)}), bf16[4,456,256]{2,1,0:T(8,128)(2,1)S(1)}, u32[]{:S(2)}, u32[]{:S(2)}) async-start(bf16[4,456,256]{2,1,0:T(8,128)(2,1)} %get-tuple-element.160), calls=%async_computation | async-start | bytes 1867776 | tf_op jit(solution)/shard_map/all_to_all | solution.py:1023
  136.3 10.9 %narrow_back.1.grad = bf16[456,4096]{1,0:T(8,128)(2,1)} custom-call(s32[5]{0:T(128)} %pad_add_fusion.scal, bf16[456,1024]{1,0:T(8,128)(2,1)} %bitcast.65, bf16[4096,1024]{1,0:T(8,128)(2,1)} %all-gather.3.cloned.1.call-done.weight), custom_call_target="tpu_custom_call" | custom-call | bytes 189440 | tf_op jit(solution)/shard_map/narrow_back/pallas_call | solution.py:572
  147.5 8.2 %all-to-all-done.refs_0_ = bf16[4,456,256]{2,1,0:T(8,128)(2,1)S(1)} async-done(((bf16[4,456,256]{2,1,0:T(8,128)(2,1)}), bf16[4,456,256]{2,1,0:T(8,128)(2,1)S(1)}, u32[]{:S(2)}, u32[]{:S(2)}) %all-to-all-start) | async-done | bytes 933920 | tf_op jit(solution)/shard_map/all_to_all | solution.py:1023
  156.7 6.4 %mix.1 = (bf16[456,1024]{1,0:T(8,128)(2,1)}, f32[456,1024]{1,0:T(8,128)}, bf16[456,1024]{1,0:T(8,128)(2,1)}) custom-call(s32[5]{0:T(128)} %pad_add_fusion.scal, bf16[4,456,256]{2,1,0:T(8,128)(2,1)} %copy-done.5, bf16[456,1024]{1,0:T(8,128)(2,1)} %bitcast.70, f32[1,1024]{1,0:T(1,128)} %get-tuple-element.165.refs_2_, f32[1,1024]{1,0:T(1,128)} %get-tuple-element.166.refs_3_, ...), custom_call_target="tpu_custom_call" | custom-call | bytes 120320 | tf_op jit(solution)/shard_map/mix/pallas_call | solution.py:327
  163.1 13.8 %widen.1 = (bf16[456,4096]{1,0:T(8,128)(2,1)}, bf16[456,4096]{1,0:T(8,128)(2,1)}) custom-call(s32[5]{0:T(128)} %pad_add_fusion.scal, bf16[456,1024]{1,0:T(8,128)(2,1)} %get-tuple-element.189.x.refs_0_, f32[1,4096]{1,0:T(1,128)} %get-tuple-element.173.bias, bf16[456,4096]{1,0:T(8,128)(2,1)} %narrow_back.1.grad, ...), custom_call_target="tpu_custom_call" | custom-call | bytes 306176 | tf_op jit(solution)/shard_map/widen/pallas_call | solution.py:359
  176.8 6.7 %outer_rows1.1 = bf16[4,512,1024]{2,1,0:T(8,128)(2,1)} custom-call(s32[5]{0:T(128)} %pad_add_fusion.scal, bf16[456,4096]{1,0:T(8,128)(2,1)} %get-tuple-element.208.left.x, bf16[456,1024]{1,0:T(8,128)(2,1)} %bitcast.66), custom_call_target="tpu_custom_call" | custom-call | bytes 65536 | tf_op jit(solution)/shard_map/outer_rows1/pallas_call | solution.py:429
  183.5 13.2 %widen_back.1 = (f32[456,1024]{1,0:T(8,128)}, bf16[456,1024]{1,0:T(8,128)(2,1)}, f32[8,1024]{1,0:T(8,128)}, f32[1,4096]{1,0:T(1,128)}) custom-call(s32[5]{0:T(128)} %pad_add_fusion.scal, bf16[456,4096]{1,0:T(8,128)(2,1)} %get-tuple-element.177.refs_0_.refs_2_, f32[456,1024]{1,0:T(8,128)} %get-tuple-element.178.refs_1_.mixed, bf16[456,1024]{1,0:T(8,128)(2,1)} %bitcast.67, ...), custom_call_target="tpu_custom_call" | custom-call | bytes 276992 | tf_op jit(solution)/shard_map/widen_back/pallas_call | solution.py:642
  196.8 11.6 %outer_two1.1 = bf16[4,128,5120]{2,1,0:T(8,128)(2,1)} custom-call(s32[5]{0:T(128)} %pad_add_fusion.scal, bf16[456,1024]{1,0:T(8,128)(2,1)} %get-tuple-element.189.x.refs_0_, bf16[456,1024]{1,0:T(8,128)(2,1)} %get-tuple-element.190.refs_1_, bf16[456,4096]{1,0:T(8,128)(2,1)} %get-tuple-element.177.refs_0_.refs_2_, ...), custom_call_target="tpu_custom_call" | custom-call | bytes 81920 | tf_op jit(solution)/shard_map/outer_two1/pallas_call | solution.py:545
  208.9 6.0 %mix_back.1 = bf16[4,456,256]{2,1,0:T(8,128)(2,1)} custom-call(s32[5]{0:T(128)} %pad_add_fusion.scal, bf16[456,1024]{1,0:T(8,128)(2,1)} %get-tuple-element.183.refs_3_.refs_0_, bf16[128,1024]{1,0:T(8,128)(2,1)} %refs_1_.1, bf16[128,1024]{1,0:T(8,128)(2,1)} %copy-done.11, bf16[128,1024]{1,0:T(8,128)(2,1)} %copy-done.9, bf16[128,1024]{1,0:T(8,128)(2,1)} %copy-done.13, ...), custom_call_target="tpu_custom_call" | custom-call | bytes 61952 | tf_op jit(solution)/shard_map/mix_back/pallas_call | solution.py:690
  218.7 8.4 %outer_rows0.1 = (bf16[512,1024]{1,0:T(8,128)(2,1)}, bf16[512,1024]{1,0:T(8,128)(2,1)}, bf16[512,1024]{1,0:T(8,128)(2,1)}, bf16[512,1024]{1,0:T(8,128)(2,1)}) custom-call(s32[5]{0:T(128)} %pad_add_fusion.scal, bf16[456,4096]{1,0:T(8,128)(2,1)} %get-tuple-element.208.left.x, bf16[456,1024]{1,0:T(8,128)(2,1)} %bitcast.68, ...), custom_call_target="tpu_custom_call" | custom-call | bytes 131072 | tf_op jit(solution)/shard_map/outer_rows0/pallas_call | solution.py:429
  227.1 12.5 %outer_two0.1 = (bf16[128,5120]{1,0:T(8,128)(2,1)}, bf16[128,5120]{1,0:T(8,128)(2,1)}, bf16[128,5120]{1,0:T(8,128)(2,1)}, bf16[128,5120]{1,0:T(8,128)(2,1)}) custom-call(s32[5]{0:T(128)} %pad_add_fusion.scal, bf16[456,1024]{1,0:T(8,128)(2,1)} %get-tuple-element.189.x.refs_0_, bf16[456,1024]{1,0:T(8,128)(2,1)} %get-tuple-element.190.refs_1_, ...), custom_call_target="tpu_custom_call" | custom-call | bytes 163840 | tf_op jit(solution)/shard_map/outer_two0/pallas_call | solution.py:545
  243.1 25.8 %attend_back.1.refs_4_ = bf16[4,456,768]{2,1,0:T(8,128)(2,1)} custom-call(s32[5]{0:T(128)} %pad_add_fusion.scal, bf16[456,768]{1,0:T(8,128)(2,1)} %get-tuple-element.143.refs_0_.refs_4_.refs_8_, bf16[456,768]{1,0:T(8,128)(2,1)} %get-tuple-element.147.refs_1_.refs_5_.refs_9_, bf16[456,768]{1,0:T(8,128)(2,1)} %get-tuple-element.151.refs_2_.refs_6_.refs_10_, ...), custom_call_target="tpu_custom_call" | custom-call | bytes 134217728 | tf_op jit(solution)/shard_map/attend_back/pallas_call | solution.py:284
  274.6 4.8 %all-to-all-start.2 = ((bf16[4,456,768]{2,1,0:T(8,128)(2,1)}), bf16[4,456,768]{2,1,0:T(8,128)(2,1)}, u32[]{:S(2)}, u32[]{:S(2)}) async-start(bf16[4,456,768]{2,1,0:T(8,128)(2,1)} %attend_back.1.refs_4_), calls=%async_computation.2 | async-start | bytes 5603328 | tf_op jit(solution)/shard_map/all_to_all | solution.py:1023
  281.5 9.1 %outer_qkv1.1 = (bf16[4,128,768]{2,1,0:T(8,128)(2,1)}, f32[1,768]{1,0:T(1,128)}) custom-call(s32[5]{0:T(128)} %pad_add_fusion.scal, bf16[456,1024]{1,0:T(8,128)(2,1)} %get-tuple-element.214.refs_0_, bf16[456,1024]{1,0:T(8,128)(2,1)} %get-tuple-element.215.refs_1_, bf16[456,1024]{1,0:T(8,128)(2,1)} %get-tuple-element.216.refs_2_, ...), custom_call_target="tpu_custom_call" | custom-call | bytes 114432 | tf_op jit(solution)/shard_map/outer_qkv1/pallas_call | solution.py:483
  290.5 5.0 %sides.4 = (bf16[128,5120]{1,0:T(8,128)(2,1)}, bf16[128,5120]{1,0:T(8,128)(2,1)}) custom-call(s32[5]{0:T(128)} %pad_add_fusion.scal, bf16[128,5120]{1,0:T(8,128)(2,1)} %get-tuple-element.191.right, bf16[128,5120]{1,0:T(8,128)(2,1)} %get-tuple-element.192.down, bf16[128,5120]{1,0:T(8,128)(2,1)} %collective-permute-done.22.passed), custom_call_target="tpu_custom_call" | custom-call | bytes 30720 | tf_op jit(solution)/shard_map/sides/pallas_call | solution.py:823
  297.6 9.9 %narrow.1 = bf16[3,146,1024]{2,1,0:T(8,128)(2,1)} custom-call(s32[5]{0:T(128)} %pad_add_fusion.scal, bf16[456,4096]{1,0:T(8,128)(2,1)} %get-tuple-element.208.left.x, f32[456,1024]{1,0:T(8,128)} %get-tuple-element.178.refs_1_.mixed, f32[1,1024]{1,0:T(1,128)} %get-tuple-element.209.bias, bf16[4096,1024]{1,0:T(8,128)(2,1)} %all-gather.3.cloned.1.call-done.weight), custom_call_target="tpu_custom_call" | custom-call | bytes 233216 | tf_op jit(solution)/shard_map/narrow/pallas_call | solution.py:391
  312.0 4.8 %collective-permute-start.33 = (bf16[512,1024]{1,0:T(8,128)(2,1)}, bf16[512,1024]{1,0:T(8,128)(2,1)}, u32[]{:S(2)}, u32[]{:S(2)}) collective-permute-start(bf16[512,1024]{1,0:T(8,128)(2,1)} %total.9), channel_id=1, source_target_pairs={{0,1},{3,2},{4,5},{7,6},{8,9},{11,10},{12,13},{15,14},{16,17},{19,... | collective-permute-start | bytes 3145736 | tf_op jit(solution)/shard_map/ppermute | solution.py:951
  316.8 8.9 %outer_qkv0.1 = (bf16[128,768]{1,0:T(8,128)(2,1)}, bf16[128,768]{1,0:T(8,128)(2,1)}, bf16[128,768]{1,0:T(8,128)(2,1)}, bf16[128,768]{1,0:T(8,128)(2,1)}) custom-call(s32[5]{0:T(128)} %pad_add_fusion.scal, bf16[456,1024]{1,0:T(8,128)(2,1)} %get-tuple-element.214.refs_0_, bf16[456,1024]{1,0:T(8,128)(2,1)} %get-tuple-element.215.refs_1_, ...), custom_call_target="tpu_custom_call" | custom-call | bytes 126720 | tf_op jit(solution)/shard_map/outer_qkv0/pallas_call | solution.py:483
  325.7 6.2 %collective-permute-done.24.refs_1_ = bf16[128,5120]{1,0:T(8,128)(2,1)S(1)} collective-permute-done((bf16[128,5120]{1,0:T(8,128)(2,1)}, bf16[128,5120]{1,0:T(8,128)(2,1)S(1)}, u32[]{:S(2)}, u32[]{:S(2)}) %collective-permute-start.24) | collective-permute-done | bytes 1310752 | tf_op jit(solution)/shard_map/ppermute | solution.py:773
  344.2 11.6 %project_back.1 = (f32[3,146,1024]{2,1,0:T(8,128)}, f32[8,1024]{1,0:T(8,128)}) custom-call(s32[5]{0:T(128)} %pad_add_fusion.scal, bf16[4,456,768]{2,1,0:T(8,128)(2,1)} %all-to-all-done.2.refs_0_, bf16[456,1024]{1,0:T(8,128)(2,1)} %bitcast.71, f32[456,1024]{1,0:T(8,128)} %get-tuple-element.225.refs_2_, f32[1,1024]{1,0:T(1,128)} %get-tuple-element.139.refs_1_.refs_3_, ...), custom_call_target="tpu_custom_call" | custom-call | bytes 215040 | tf_op jit(solution)/shard_map/project_back/pallas_call | solution.py:746
  360.8 4.9 %total.12.refs_0_ = bf16[512,1024]{1,0:T(8,128)(2,1)} custom-call(s32[5]{0:T(128)} %pad_add_fusion.scal, bf16[512,1024]{1,0:T(8,128)(2,1)} %get-tuple-element.211.refs_0_, bf16[512,1024]{1,0:T(8,128)(2,1)} %collective-permute-done.26.refs_1_, bf16[512,1024]{1,0:T(8,128)(2,1)} %collective-permute-done.27.refs_2_, ...), custom_call_target="tpu_custom_call" | custom-call | tf_op jit(solution)/shard_map/total/pallas_call | solution.py:874
  367.4 7.0 %collective-permute-start.34 = (bf16[64,5120]{1,0:T(8,128)(2,1)S(1)}, bf16[64,5120]{1,0:T(8,128)(2,1)S(1)}, u32[]{:S(2)}, u32[]{:S(2)}) collective-permute-start(bf16[64,5120]{1,0:T(8,128)(2,1)S(1)} %copy-done.17), channel_id=1, source_target_pairs={{0,1},{3,2},{4,5},{7,6},{8,9},{11,10},{12,13},{15,14},{16,17},{19,... | collective-permute-start | bytes 1966088 | tf_op jit(solution)/shard_map/ppermute | solution.py:951
  412.0 24.8 %collective-permute-done.41.refs_1_ = bf16[512,1024]{1,0:T(8,128)(2,1)} collective-permute-done((bf16[512,1024]{1,0:T(8,128)(2,1)}, bf16[512,1024]{1,0:T(8,128)(2,1)}, u32[]{:S(2)}, u32[]{:S(2)}) %collective-permute-start.41) | collective-permute-done | bytes 1048608 | tf_op jit(solution)/shard_map/ppermute | solution.py:960
  452.9 13.9 %collective-permute-done.43.refs_3_ = bf16[64,5120]{1,0:T(8,128)(2,1)S(1)} collective-permute-done((bf16[64,5120]{1,0:T(8,128)(2,1)}, bf16[64,5120]{1,0:T(8,128)(2,1)S(1)}, u32[]{:S(2)}, u32[]{:S(2)}) %collective-permute-start.43) | collective-permute-done | bytes 655392 | tf_op jit(solution)/shard_map/ppermute | solution.py:960
  (195 shorter events, 136.9 us)
Async XLA Ops:
  7.2 129.1 %all-gather.3.cloned.1.call-start = ((), (), s32[]{:S(2)}) async-start(), calls=%async_computation.4 | async-start | bytes 9437184 | tf_op jit(solution)/shard_map/all_gather | solution.py:1073
  7.2 33.1 %collective-permute-start.2 = (bf16[3,146,1024]{2,1,0:T(8,128)(2,1)}, bf16[3,146,1024]{2,1,0:T(8,128)(2,1)}, u32[]{:S(2)}, u32[]{:S(2)}) collective-permute-start(bf16[3,146,1024]{2,1,0:T(8,128)(2,1)} %param.16), channel_id=1, source_target_pairs={{1,0},{2,1},{3,2},{5,4},{6,5},{7,6},{9,8},{10,9},{11,10},{13,12},{... | collective-permute-start | bytes 2691080 | tf_op jit(solution)/shard_map/ppermute | solution.py:1007
  8.5 31.8 %collective-permute-start = (bf16[3,146,1024]{2,1,0:T(8,128)(2,1)}, bf16[3,146,1024]{2,1,0:T(8,128)(2,1)}, u32[]{:S(2)}, u32[]{:S(2)}) collective-permute-start(bf16[3,146,1024]{2,1,0:T(8,128)(2,1)} %param.16), channel_id=1, source_target_pairs={{0,1},{1,2},{2,3},{4,5},{5,6},{6,7},{8,9},{9,10},{10,11},{12,13},{... | collective-permute-start | bytes 2691080 | tf_op jit(solution)/shard_map/ppermute | solution.py:1006
  17.8 21.2 %collective-permute-start.5 = (bf16[144,3072]{1,0:T(8,128)(2,1)S(1)}, bf16[144,3072]{1,0:T(8,128)(2,1)S(1)}, u32[]{:S(2)}, u32[]{:S(2)}) collective-permute-start(bf16[144,3072]{1,0:T(8,128)(2,1)S(1)} %fusion.2.refs_0_.refs_5_.refs_4_), channel_id=1, source_target_pairs={{0,16},{4,20},{8,24},{12,28},{16,0},{20,4},{24,8},{28,12},{1,17},{... | collective-permute-start | bytes 2654216 | tf_op jit(solution)/shard_map/ppermute | solution.py:773
  19.8 20.5 %collective-permute-start.4 = (bf16[144,3072]{1,0:T(8,128)(2,1)S(1)}, bf16[144,3072]{1,0:T(8,128)(2,1)S(1)}, u32[]{:S(2)}, u32[]{:S(2)}) collective-permute-start(bf16[144,3072]{1,0:T(8,128)(2,1)S(1)} %fusion.2.refs_0_.refs_5_.refs_4_), channel_id=1, source_target_pairs={{0,8},{4,12},{8,0},{12,4},{16,24},{20,28},{24,16},{28,20},{1,9},{5... | collective-permute-start | bytes 2654216 | tf_op jit(solution)/shard_map/ppermute | solution.py:773
  40.4 122.7 %all-gather.5.cloned.1.call-start = ((), (), s32[]{:S(2)}) async-start(), calls=%async_computation.5 | async-start | bytes 9437184 | tf_op jit(solution)/shard_map/all_gather | solution.py:1073
  41.2 27.4 %collective-permute-start.3 = (bf16[3,146,1024]{2,1,0:T(8,128)(2,1)}, bf16[3,146,1024]{2,1,0:T(8,128)(2,1)}, u32[]{:S(2)}, u32[]{:S(2)}) collective-permute-start(bf16[3,146,1024]{2,1,0:T(8,128)(2,1)} %collective-permute-done.2), channel_id=1, source_target_pairs={{1,0},{2,1},{5,4},{6,5},{9,8},{10,9},{13,12},{14,13},{17,16},{18,1... | collective-permute-start | bytes 2691080 | tf_op jit(solution)/shard_map/ppermute | solution.py:1007
  42.5 26.1 %collective-permute-start.1 = (bf16[3,146,1024]{2,1,0:T(8,128)(2,1)}, bf16[3,146,1024]{2,1,0:T(8,128)(2,1)}, u32[]{:S(2)}, u32[]{:S(2)}) collective-permute-start(bf16[3,146,1024]{2,1,0:T(8,128)(2,1)} %collective-permute-done), channel_id=1, source_target_pairs={{1,2},{2,3},{5,6},{6,7},{9,10},{10,11},{13,14},{14,15},{17,18},{18... | collective-permute-start | bytes 2691080 | tf_op jit(solution)/shard_map/ppermute | solution.py:1006
  44.1 24.4 %collective-permute-start.9 = (bf16[144,3072]{1,0:T(8,128)(2,1)S(1)}, bf16[144,3072]{1,0:T(8,128)(2,1)}, u32[]{:S(2)}, u32[]{:S(2)}) collective-permute-start(bf16[144,3072]{1,0:T(8,128)(2,1)S(1)} %broadcast_select_fusion), channel_id=1, source_target_pairs={{0,8},{4,20},{8,0},{12,28},{16,24},{20,4},{24,16},{28,12},{1,9},{5... | collective-permute-start | bytes 2654216 | tf_op jit(solution)/shard_map/ppermute | solution.py:777
  45.7 27.1 %collective-permute-start.6 = (bf16[144,3072]{1,0:T(8,128)(2,1)S(1)}, bf16[144,3072]{1,0:T(8,128)(2,1)}, u32[]{:S(2)}, u32[]{:S(2)}) collective-permute-start(bf16[144,3072]{1,0:T(8,128)(2,1)S(1)} %fusion.2.refs_0_.refs_5_.refs_4_), channel_id=1, source_target_pairs={{0,4},{4,0},{8,12},{12,8},{16,20},{20,16},{24,28},{28,24},{1,5},{5... | collective-permute-start | bytes 2654216 | tf_op jit(solution)/shard_map/ppermute | solution.py:773
  71.5 32.1 %collective-permute-start.12 = (bf16[3,146,1024]{2,1,0:T(8,128)(2,1)}, bf16[3,146,1024]{2,1,0:T(8,128)(2,1)}, u32[]{:S(2)}, u32[]{:S(2)}) collective-permute-start(bf16[3,146,1024]{2,1,0:T(8,128)(2,1)} %collective-permute-done.3), channel_id=1, source_target_pairs={{1,0},{5,4},{9,8},{13,12},{17,16},{21,20},{25,24},{29,28}} | collective-permute-start | bytes 2691080 | tf_op jit(solution)/shard_map/ppermute | solution.py:1007
  72.8 30.9 %collective-permute-start.11 = (bf16[3,146,1024]{2,1,0:T(8,128)(2,1)}, bf16[3,146,1024]{2,1,0:T(8,128)(2,1)}, u32[]{:S(2)}, u32[]{:S(2)}) collective-permute-start(bf16[3,146,1024]{2,1,0:T(8,128)(2,1)} %collective-permute-done.1), channel_id=1, source_target_pairs={{2,3},{6,7},{10,11},{14,15},{18,19},{22,23},{26,27},{30,31}} | collective-permute-start | bytes 2691080 | tf_op jit(solution)/shard_map/ppermute | solution.py:1006
  101.2 24.8 %collective-permute-start.15 = (bf16[128,1024]{1,0:T(8,128)(2,1)S(1)}, bf16[128,1024]{1,0:T(8,128)(2,1)S(1)}, u32[]{:S(2)}, u32[]{:S(2)}) collective-permute-start(bf16[128,1024]{1,0:T(8,128)(2,1)S(1)} %copy-done.10), channel_id=1, source_target_pairs={{0,4},{4,0},{8,12},{12,8},{16,20},{20,16},{24,28},{28,24},{1,5},{5... | collective-permute-start | bytes 786440 | tf_op jit(solution)/shard_map/ppermute | solution.py:773
  101.6 24.4 %collective-permute-start.14 = (bf16[128,1024]{1,0:T(8,128)(2,1)S(1)}, bf16[128,1024]{1,0:T(8,128)(2,1)S(1)}, u32[]{:S(2)}, u32[]{:S(2)}) collective-permute-start(bf16[128,1024]{1,0:T(8,128)(2,1)S(1)} %copy-done.10), channel_id=1, source_target_pairs={{0,16},{4,20},{8,24},{12,28},{16,0},{20,4},{24,8},{28,12},{1,17},{... | collective-permute-start | bytes 786440 | tf_op jit(solution)/shard_map/ppermute | solution.py:773
  102.0 24.1 %collective-permute-start.13 = (bf16[128,1024]{1,0:T(8,128)(2,1)S(1)}, bf16[128,1024]{1,0:T(8,128)(2,1)S(1)}, u32[]{:S(2)}, u32[]{:S(2)}) collective-permute-start(bf16[128,1024]{1,0:T(8,128)(2,1)S(1)} %copy-done.10), channel_id=1, source_target_pairs={{0,8},{4,12},{8,0},{12,4},{16,24},{20,28},{24,16},{28,20},{1,9},{5... | collective-permute-start | bytes 786440 | tf_op jit(solution)/shard_map/ppermute | solution.py:773
  126.0 29.6 %all-to-all-start = ((bf16[4,456,256]{2,1,0:T(8,128)(2,1)}), bf16[4,456,256]{2,1,0:T(8,128)(2,1)S(1)}, u32[]{:S(2)}, u32[]{:S(2)}) async-start(bf16[4,456,256]{2,1,0:T(8,128)(2,1)} %get-tuple-element.160), calls=%async_computation | async-start | bytes 1867776 | tf_op jit(solution)/shard_map/all_to_all | solution.py:1023
  214.9 27.2 %all-to-all-start.1 = ((bf16[4,456,256]{2,1,0:T(8,128)(2,1)}), bf16[4,456,256]{2,1,0:T(8,128)(2,1)S(1)}, u32[]{:S(2)}, u32[]{:S(2)}) async-start(bf16[4,456,256]{2,1,0:T(8,128)(2,1)} %mix_back.1), calls=%async_computation.1 | async-start | bytes 1867776 | tf_op jit(solution)/shard_map/all_to_all | solution.py:1023
  239.6 35.0 %collective-permute-start.22 = (bf16[128,5120]{1,0:T(8,128)(2,1)}, bf16[128,5120]{1,0:T(8,128)(2,1)}, u32[]{:S(2)}, u32[]{:S(2)}) collective-permute-start(bf16[128,5120]{1,0:T(8,128)(2,1)} %get-tuple-element.193), channel_id=1, source_target_pairs={{0,8},{4,20},{8,0},{12,28},{16,24},{20,4},{24,16},{28,12},{1,9},{5... | collective-permute-start | bytes 3932168 | tf_op jit(solution)/shard_map/ppermute | solution.py:777
  241.2 27.7 %collective-permute-start.23 = (bf16[512,1024]{1,0:T(8,128)(2,1)}, bf16[512,1024]{1,0:T(8,128)(2,1)S(1)}, u32[]{:S(2)}, u32[]{:S(2)}) collective-permute-start(bf16[512,1024]{1,0:T(8,128)(2,1)} %get-tuple-element.188), channel_id=1, source_target_pairs={{0,8},{4,20},{8,0},{12,28},{16,24},{20,4},{24,16},{28,12},{1,9},{5... | collective-permute-start | bytes 3145736 | tf_op jit(solution)/shard_map/ppermute | solution.py:777
  274.6 69.6 %all-to-all-start.2 = ((bf16[4,456,768]{2,1,0:T(8,128)(2,1)}), bf16[4,456,768]{2,1,0:T(8,128)(2,1)}, u32[]{:S(2)}, u32[]{:S(2)}) async-start(bf16[4,456,768]{2,1,0:T(8,128)(2,1)} %attend_back.1.refs_4_), calls=%async_computation.2 | async-start | bytes 5603328 | tf_op jit(solution)/shard_map/all_to_all | solution.py:1023
  279.4 28.0 %collective-permute-start.26 = (bf16[512,1024]{1,0:T(8,128)(2,1)}, bf16[512,1024]{1,0:T(8,128)(2,1)}, u32[]{:S(2)}, u32[]{:S(2)}) collective-permute-start(bf16[512,1024]{1,0:T(8,128)(2,1)} %get-tuple-element.201), channel_id=1, source_target_pairs={{0,8},{4,12},{8,0},{12,4},{16,24},{20,28},{24,16},{28,20},{1,9},{5... | collective-permute-start | bytes 3145736 | tf_op jit(solution)/shard_map/ppermute | solution.py:773
  281.1 26.4 %collective-permute-start.27 = (bf16[512,1024]{1,0:T(8,128)(2,1)}, bf16[512,1024]{1,0:T(8,128)(2,1)}, u32[]{:S(2)}, u32[]{:S(2)}) collective-permute-start(bf16[512,1024]{1,0:T(8,128)(2,1)} %get-tuple-element.202), channel_id=1, source_target_pairs={{0,16},{4,20},{8,24},{12,28},{16,0},{20,4},{24,8},{28,12},{1,17},{... | collective-permute-start | bytes 3145736 | tf_op jit(solution)/shard_map/ppermute | solution.py:773
  295.5 36.5 %collective-permute-start.24 = (bf16[128,5120]{1,0:T(8,128)(2,1)}, bf16[128,5120]{1,0:T(8,128)(2,1)S(1)}, u32[]{:S(2)}, u32[]{:S(2)}) collective-permute-start(bf16[128,5120]{1,0:T(8,128)(2,1)} %get-tuple-element.206), channel_id=1, source_target_pairs={{0,8},{4,12},{8,0},{12,4},{16,24},{20,28},{24,16},{28,20},{1,9},{5... | collective-permute-start | bytes 3932168 | tf_op jit(solution)/shard_map/ppermute | solution.py:773
  296.8 36.6 %collective-permute-start.25 = (bf16[128,5120]{1,0:T(8,128)(2,1)}, bf16[128,5120]{1,0:T(8,128)(2,1)}, u32[]{:S(2)}, u32[]{:S(2)}) collective-permute-start(bf16[128,5120]{1,0:T(8,128)(2,1)} %get-tuple-element.207), channel_id=1, source_target_pairs={{0,16},{4,20},{8,24},{12,28},{16,0},{20,4},{24,8},{28,12},{1,17},{... | collective-permute-start | bytes 3932168 | tf_op jit(solution)/shard_map/ppermute | solution.py:773
  312.0 48.2 %collective-permute-start.33 = (bf16[512,1024]{1,0:T(8,128)(2,1)}, bf16[512,1024]{1,0:T(8,128)(2,1)}, u32[]{:S(2)}, u32[]{:S(2)}) collective-permute-start(bf16[512,1024]{1,0:T(8,128)(2,1)} %total.9), channel_id=1, source_target_pairs={{0,1},{3,2},{4,5},{7,6},{8,9},{11,10},{12,13},{15,14},{16,17},{19,... | collective-permute-start | bytes 3145736 | tf_op jit(solution)/shard_map/ppermute | solution.py:951
  336.5 24.3 %collective-permute-start.32 = (bf16[64,5120]{1,0:T(8,128)(2,1)}, bf16[64,5120]{1,0:T(8,128)(2,1)S(1)}, u32[]{:S(2)}, u32[]{:S(2)}) collective-permute-start(bf16[64,5120]{1,0:T(8,128)(2,1)} %total.10), channel_id=1, source_target_pairs={{0,1},{3,2},{4,5},{7,6},{8,9},{11,10},{12,13},{15,14},{16,17},{19,... | collective-permute-start | bytes 1966088 | tf_op jit(solution)/shard_map/ppermute | solution.py:951
  365.7 33.4 %collective-permute-start.39 = (bf16[512,1024]{1,0:T(8,128)(2,1)}, bf16[512,1024]{1,0:T(8,128)(2,1)}, u32[]{:S(2)}, u32[]{:S(2)}) collective-permute-start(bf16[512,1024]{1,0:T(8,128)(2,1)} %total.12.refs_0_), channel_id=1, source_target_pairs={{1,2},{2,1},{5,6},{6,5},{9,10},{10,9},{13,14},{14,13},{17,18},{18,... | collective-permute-start | bytes 3145736 | tf_op jit(solution)/shard_map/ppermute | solution.py:955
  395.7 48.9 %all-to-all-start.3 = ((bf16[4,144,768]{2,1,0:T(8,128)(2,1)}), bf16[4,144,768]{2,1,0:T(8,128)(2,1)S(1)}, u32[]{:S(2)}, u32[]{:S(2)}) async-start(bf16[4,144,768]{2,1,0:T(8,128)(2,1)} %copies.1), calls=%async_computation.3 | async-start | bytes 1769472 | tf_op jit(solution)/shard_map/all_to_all | solution.py:1023
  403.6 33.1 %collective-permute-start.41 = (bf16[512,1024]{1,0:T(8,128)(2,1)}, bf16[512,1024]{1,0:T(8,128)(2,1)}, u32[]{:S(2)}, u32[]{:S(2)}) collective-permute-start(bf16[512,1024]{1,0:T(8,128)(2,1)} %total.15.refs_0_), channel_id=1, source_target_pairs={{1,0},{2,3},{5,4},{6,7},{9,8},{10,11},{13,12},{14,15},{17,16},{18,... | collective-permute-start | bytes 3145736 | tf_op jit(solution)/shard_map/ppermute | solution.py:960
  406.4 34.1 %collective-permute-start.40 = (bf16[64,5120]{1,0:T(8,128)(2,1)S(1)}, bf16[64,5120]{1,0:T(8,128)(2,1)}, u32[]{:S(2)}, u32[]{:S(2)}) collective-permute-start(bf16[64,5120]{1,0:T(8,128)(2,1)S(1)} %copy-done.7), channel_id=1, source_target_pairs={{1,2},{2,1},{5,6},{6,5},{9,10},{10,9},{13,14},{14,13},{17,18},{18,... | collective-permute-start | bytes 1966088 | tf_op jit(solution)/shard_map/ppermute | solution.py:955
  410.7 42.3 %collective-permute-start.42 = (bf16[64,5120]{1,0:T(8,128)(2,1)}, bf16[64,5120]{1,0:T(8,128)(2,1)}, u32[]{:S(2)}, u32[]{:S(2)}) collective-permute-start(bf16[64,5120]{1,0:T(8,128)(2,1)} %total.16.refs_0_), channel_id=1, source_target_pairs={{1,0},{2,3},{5,4},{6,7},{9,8},{10,11},{13,12},{14,15},{17,16},{18,... | collective-permute-start | bytes 1966088 | tf_op jit(solution)/shard_map/ppermute | solution.py:960
  443.2 23.6 %collective-permute-start.43 = (bf16[64,5120]{1,0:T(8,128)(2,1)}, bf16[64,5120]{1,0:T(8,128)(2,1)S(1)}, u32[]{:S(2)}, u32[]{:S(2)}) collective-permute-start(bf16[64,5120]{1,0:T(8,128)(2,1)} %total.17.refs_1_), channel_id=1, source_target_pairs={{1,0},{2,3},{5,4},{6,7},{9,8},{10,11},{13,12},{14,15},{17,16},{18,... | collective-permute-start | bytes 1966088 | tf_op jit(solution)/shard_map/ppermute | solution.py:960
  (48 other events, 464.5 us)
Sparse Core Ops, SparseCore 0:
  40.5 58.3 all-gather.2
  100.8 57.7 all-gather.4
where the time goes:
time: 483 us; the launch traced here: 479 us
  Pallas kernels  255 us (53%)
  waiting for transfers between devices  102 us (21%)
  starting transfers between devices  79.8 us (17%)
  local copies, waits for them, and re-layouts  20.1 us (4%)
  between operations  14.5 us (3%)
  other arithmetic  7 us (1%)
    ppermute x3, waiting for transfers between devices, outward(): return lax.ppermute(value, 'seq', [(1, 0), (last - 1, last)])  40.3 us
    pallas_call x9, Pallas kernels, total(): call(total_body, (steps,), specs, pl.BlockSpec(block, lambda n, s: (n, 0)...  32 us
    ppermute x24, waiting for transfers between devices, flip(): return lax.ppermute(value, 'fsdp', [(i, i ^ bit) for i in range(PIECES)])  29 us
    pallas_call x1, Pallas kernels, attend_back(): call(functools.partial(attend_back_body, n_seq=n_seq, unit=unit, pairs=pa...  25.8 us
    pallas_call x4, Pallas kernels, project(): call(functools.partial(project_body, rows=rows, unit=unit), (3,), [whole(...  25.6 us
    pallas_call x2, Pallas kernels, outer_two(): call(functools.partial(outer_two_body, offset=offset, width=width, first=...  24.1 us
    ppermute x5, waiting for transfers between devices, flip_mixed(): lax.ppermute(value, 'fsdp', [(i, i ^ (4 if i & 1 else 2)) for i in range(...  22.9 us
    all_to_all x4, starting transfers between devices, exchange(): return lax.all_to_all(value, 'seq', 0, 0, tiled=True)  18.6 us
  transfers between devices with their start and end apart: 50, of which 13 were waited for; matrix products, arithmetic and copies ran while one was open for 4% of the time, Pallas kernels for 45%

commit v1 on v0

--- a/solution.py
+++ b/solution.py
@@ -834,7 +834,7 @@
 
 
 def row_steps(value):
-    return 4 if value.shape[0] % 64 == 0 else 1
+    return 2 if value.shape[0] % 64 == 0 else 1
 
 
 def sides(scal, summed, passed):
@@ -863,7 +863,7 @@
 def total(scal, parts, half=None):
     rows, wide = parts[0].shape
     rows = rows if half is None else rows // 2
-    steps = max(1, min(4, rows // 32)) if rows % 32 == 0 else 1
+    steps = max(1, min(2, rows // 32)) if rows % 32 == 0 else 1
     block = (rows // steps, wide)
     specs = [
         pl.BlockSpec(

time: 483 us -> 480 us (level)
  Pallas kernels: 255 us -> 248 us
  waiting for transfers between devices: 102 us -> 107 us
  transfers between devices with their start and end apart: 50 -> 50, of which waited for: 13 -> 14; matrix products, arithmetic and copies ran while one was open for 4% -> 4% of each run, Pallas kernels for 45% -> 44%
where the time goes in v1:
time: 480 us; the launch traced here: 477 us
  Pallas kernels  248 us (52%)
  waiting for transfers between devices  107 us (22%)
  starting transfers between devices  79.8 us (17%)
  local copies, waits for them, and re-layouts  20.1 us (4%)
  between operations  14.5 us (3%)
  other arithmetic  7 us (1%)
    ppermute x3, waiting for transfers between devices, outward(): return lax.ppermute(value, 'seq', [(1, 0), (last - 1, last)])  41.5 us
    ppermute x24, waiting for transfers between devices, flip(): return lax.ppermute(value, 'fsdp', [(i, i ^ bit) for i in range(PIECES)])  31 us
    pallas_call x9, Pallas kernels, total(): call(total_body, (steps,), specs, pl.BlockSpec(block, lambda n, s: (n, 0)...  28.8 us
    pallas_call x1, Pallas kernels, attend_back(): call(functools.partial(attend_back_body, n_seq=n_seq, unit=unit, pairs=pa...  25.8 us
    pallas_call x4, Pallas kernels, project(): call(functools.partial(project_body, rows=rows, unit=unit), (3,), [whole(...  25.6 us
    pallas_call x2, Pallas kernels, outer_two(): call(functools.partial(outer_two_body, offset=offset, width=width, first=...  24.1 us
    ppermute x5, waiting for transfers between devices, flip_mixed(): lax.ppermute(value, 'fsdp', [(i, i ^ (4 if i & 1 else 2)) for i in range(...  22.9 us
    all_to_all x4, starting transfers between devices, exchange(): return lax.all_to_all(value, 'seq', 0, 0, tiled=True)  18.6 us
  transfers between devices with their start and end apart: 50, of which 14 were waited for; matrix products, arithmetic and copies ran while one was open for 4% of the time, Pallas kernels for 44%

profile of v1, /device:TPU:0, one launch (start us, length us, event | category | flops | bytes accessed | tf_op | source)
XLA Modules:
  0.0 476.6 jit_solution(8664811639665664199)
XLA Ops:
  8.5 6.5 %collective-permute-start = (bf16[3,146,1024]{2,1,0:T(8,128)(2,1)}, bf16[3,146,1024]{2,1,0:T(8,128)(2,1)}, u32[]{:S(2)}, u32[]{:S(2)}) collective-permute-start(bf16[3,146,1024]{2,1,0:T(8,128)(2,1)} %param.16), channel_id=1, source_target_pairs={{0,1},{1,2},{2,3},{4,5},{5,6},{6,7},{8,9},{9,10},{10,11},{12,13},{... | collective-permute-start | bytes 2691080 | tf_op jit(solution)/shard_map/ppermute | solution.py:1006
  21.3 17.7 %collective-permute-done.5.refs_4_.refs_9_.refs_8_ = bf16[144,3072]{1,0:T(8,128)(2,1)S(1)} collective-permute-done((bf16[144,3072]{1,0:T(8,128)(2,1)S(1)}, bf16[144,3072]{1,0:T(8,128)(2,1)S(1)}, u32[]{:S(2)}, u32[]{:S(2)}) %collective-permute-start.5) | collective-permute-done | bytes 884768 | tf_op jit(solution)/shard_map/ppermute | solution.py:773
  45.7 22.9 %collective-permute-done.9.refs_6_.refs_11_.refs_10_ = bf16[144,3072]{1,0:T(8,128)(2,1)} collective-permute-done((bf16[144,3072]{1,0:T(8,128)(2,1)S(1)}, bf16[144,3072]{1,0:T(8,128)(2,1)}, u32[]{:S(2)}, u32[]{:S(2)}) %collective-permute-start.9) | collective-permute-done | bytes 884768 | tf_op jit(solution)/shard_map/ppermute | solution.py:777
  77.8 6.3 %project.4 = (bf16[456,768]{1,0:T(8,128)(2,1)}, bf16[456,1024]{1,0:T(8,128)(2,1)}) custom-call(s32[5]{0:T(128)} %pad_add_fusion.scal, bf16[456,1024]{1,0:T(8,128)(2,1)} %bitcast.69, f32[1,1024]{1,0:T(1,128)} %get-tuple-element.139.refs_1_.refs_3_, f32[1,1024]{1,0:T(1,128)} %get-tuple-element.140.refs_2_, f32[1,1024]{1,0:T(1,128)} %get-tuple-element.141.refs_3_, ...), custom_call_target="tpu_custom_call" | custom-call | bytes 53760 | tf_op jit(solution)/shard_map/project/pallas_call | solution.py:114
  88.4 6.4 %project.5 = (bf16[456,768]{1,0:T(8,128)(2,1)}, bf16[456,1024]{1,0:T(8,128)(2,1)}) custom-call(s32[5]{0:T(128)} %pad_add_fusion.scal, bf16[456,1024]{1,0:T(8,128)(2,1)} %bitcast.74, f32[1,1024]{1,0:T(1,128)} %get-tuple-element.139.refs_1_.refs_3_, f32[1,1024]{1,0:T(1,128)} %get-tuple-element.140.refs_2_, f32[1,1024]{1,0:T(1,128)} %get-tuple-element.141.refs_3_, ...), custom_call_target="tpu_custom_call" | custom-call | bytes 53760 | tf_op jit(solution)/shard_map/project/pallas_call | solution.py:114
  94.7 6.4 %project.6 = (bf16[456,768]{1,0:T(8,128)(2,1)}, bf16[456,1024]{1,0:T(8,128)(2,1)}) custom-call(s32[5]{0:T(128)} %pad_add_fusion.scal, bf16[456,1024]{1,0:T(8,128)(2,1)} %bitcast.72, f32[1,1024]{1,0:T(1,128)} %get-tuple-element.139.refs_1_.refs_3_, f32[1,1024]{1,0:T(1,128)} %get-tuple-element.140.refs_2_, f32[1,1024]{1,0:T(1,128)} %get-tuple-element.141.refs_3_, ...), custom_call_target="tpu_custom_call" | custom-call | bytes 53760 | tf_op jit(solution)/shard_map/project/pallas_call | solution.py:114
  106.0 6.5 %project.7 = (bf16[456,768]{1,0:T(8,128)(2,1)}, bf16[456,1024]{1,0:T(8,128)(2,1)}) custom-call(s32[5]{0:T(128)} %pad_add_fusion.scal, bf16[456,1024]{1,0:T(8,128)(2,1)} %bitcast.73, f32[1,1024]{1,0:T(1,128)} %get-tuple-element.139.refs_1_.refs_3_, f32[1,1024]{1,0:T(1,128)} %get-tuple-element.140.refs_2_, f32[1,1024]{1,0:T(1,128)} %get-tuple-element.141.refs_3_, ...), custom_call_target="tpu_custom_call" | custom-call | bytes 53760 | tf_op jit(solution)/shard_map/project/pallas_call | solution.py:114
  112.5 13.5 %attend.1 = (bf16[4,456,256]{2,1,0:T(8,128)(2,1)}, f32[3,2,608,128]{3,2,1,0:T(8,128)}) custom-call(s32[5]{0:T(128)} %pad_add_fusion.scal, bf16[456,768]{1,0:T(8,128)(2,1)} %get-tuple-element.143.refs_0_.refs_4_.refs_8_, bf16[456,768]{1,0:T(8,128)(2,1)} %get-tuple-element.147.refs_1_.refs_5_.refs_9_, ...), custom_call_target="tpu_custom_call" | custom-call | bytes 87552 | tf_op jit(solution)/shard_map/attend/pallas_call | solution.py:212
  126.0 6.4 %all-to-all-start = ((bf16[4,456,256]{2,1,0:T(8,128)(2,1)}), bf16[4,456,256]{2,1,0:T(8,128)(2,1)S(1)}, u32[]{:S(2)}, u32[]{:S(2)}) async-start(bf16[4,456,256]{2,1,0:T(8,128)(2,1)} %get-tuple-element.160), calls=%async_computation | async-start | bytes 1867776 | tf_op jit(solution)/shard_map/all_to_all | solution.py:1023
  136.3 10.9 %narrow_back.1.grad = bf16[456,4096]{1,0:T(8,128)(2,1)} custom-call(s32[5]{0:T(128)} %pad_add_fusion.scal, bf16[456,1024]{1,0:T(8,128)(2,1)} %bitcast.65, bf16[4096,1024]{1,0:T(8,128)(2,1)} %all-gather.3.cloned.1.call-done.weight), custom_call_target="tpu_custom_call" | custom-call | bytes 189440 | tf_op jit(solution)/shard_map/narrow_back/pallas_call | solution.py:572
  147.5 8.2 %all-to-all-done.refs_0_ = bf16[4,456,256]{2,1,0:T(8,128)(2,1)S(1)} async-done(((bf16[4,456,256]{2,1,0:T(8,128)(2,1)}), bf16[4,456,256]{2,1,0:T(8,128)(2,1)S(1)}, u32[]{:S(2)}, u32[]{:S(2)}) %all-to-all-start) | async-done | bytes 933920 | tf_op jit(solution)/shard_map/all_to_all | solution.py:1023
  156.7 6.4 %mix.1 = (bf16[456,1024]{1,0:T(8,128)(2,1)}, f32[456,1024]{1,0:T(8,128)}, bf16[456,1024]{1,0:T(8,128)(2,1)}) custom-call(s32[5]{0:T(128)} %pad_add_fusion.scal, bf16[4,456,256]{2,1,0:T(8,128)(2,1)} %copy-done.5, bf16[456,1024]{1,0:T(8,128)(2,1)} %bitcast.70, f32[1,1024]{1,0:T(1,128)} %get-tuple-element.165.refs_2_, f32[1,1024]{1,0:T(1,128)} %get-tuple-element.166.refs_3_, ...), custom_call_target="tpu_custom_call" | custom-call | bytes 120320 | tf_op jit(solution)/shard_map/mix/pallas_call | solution.py:327
  163.1 13.8 %widen.1 = (bf16[456,4096]{1,0:T(8,128)(2,1)}, bf16[456,4096]{1,0:T(8,128)(2,1)}) custom-call(s32[5]{0:T(128)} %pad_add_fusion.scal, bf16[456,1024]{1,0:T(8,128)(2,1)} %get-tuple-element.189.x.refs_0_, f32[1,4096]{1,0:T(1,128)} %get-tuple-element.173.bias, bf16[456,4096]{1,0:T(8,128)(2,1)} %narrow_back.1.grad, ...), custom_call_target="tpu_custom_call" | custom-call | bytes 306176 | tf_op jit(solution)/shard_map/widen/pallas_call | solution.py:359
  176.8 6.7 %outer_rows1.1 = bf16[4,512,1024]{2,1,0:T(8,128)(2,1)} custom-call(s32[5]{0:T(128)} %pad_add_fusion.scal, bf16[456,4096]{1,0:T(8,128)(2,1)} %get-tuple-element.208.left.x, bf16[456,1024]{1,0:T(8,128)(2,1)} %bitcast.66), custom_call_target="tpu_custom_call" | custom-call | bytes 65536 | tf_op jit(solution)/shard_map/outer_rows1/pallas_call | solution.py:429
  183.5 13.2 %widen_back.1 = (f32[456,1024]{1,0:T(8,128)}, bf16[456,1024]{1,0:T(8,128)(2,1)}, f32[8,1024]{1,0:T(8,128)}, f32[1,4096]{1,0:T(1,128)}) custom-call(s32[5]{0:T(128)} %pad_add_fusion.scal, bf16[456,4096]{1,0:T(8,128)(2,1)} %get-tuple-element.177.refs_0_.refs_2_, f32[456,1024]{1,0:T(8,128)} %get-tuple-element.178.refs_1_.mixed, bf16[456,1024]{1,0:T(8,128)(2,1)} %bitcast.67, ...), custom_call_target="tpu_custom_call" | custom-call | bytes 276992 | tf_op jit(solution)/shard_map/widen_back/pallas_call | solution.py:642
  196.8 11.6 %outer_two1.1 = bf16[4,128,5120]{2,1,0:T(8,128)(2,1)} custom-call(s32[5]{0:T(128)} %pad_add_fusion.scal, bf16[456,1024]{1,0:T(8,128)(2,1)} %get-tuple-element.189.x.refs_0_, bf16[456,1024]{1,0:T(8,128)(2,1)} %get-tuple-element.190.refs_1_, bf16[456,4096]{1,0:T(8,128)(2,1)} %get-tuple-element.177.refs_0_.refs_2_, ...), custom_call_target="tpu_custom_call" | custom-call | bytes 81920 | tf_op jit(solution)/shard_map/outer_two1/pallas_call | solution.py:545
  208.9 6.0 %mix_back.1 = bf16[4,456,256]{2,1,0:T(8,128)(2,1)} custom-call(s32[5]{0:T(128)} %pad_add_fusion.scal, bf16[456,1024]{1,0:T(8,128)(2,1)} %get-tuple-element.183.refs_3_.refs_0_, bf16[128,1024]{1,0:T(8,128)(2,1)} %refs_1_.1, bf16[128,1024]{1,0:T(8,128)(2,1)} %copy-done.11, bf16[128,1024]{1,0:T(8,128)(2,1)} %copy-done.9, bf16[128,1024]{1,0:T(8,128)(2,1)} %copy-done.13, ...), custom_call_target="tpu_custom_call" | custom-call | bytes 61952 | tf_op jit(solution)/shard_map/mix_back/pallas_call | solution.py:690
  218.7 8.4 %outer_rows0.1 = (bf16[512,1024]{1,0:T(8,128)(2,1)}, bf16[512,1024]{1,0:T(8,128)(2,1)}, bf16[512,1024]{1,0:T(8,128)(2,1)}, bf16[512,1024]{1,0:T(8,128)(2,1)}) custom-call(s32[5]{0:T(128)} %pad_add_fusion.scal, bf16[456,4096]{1,0:T(8,128)(2,1)} %get-tuple-element.208.left.x, bf16[456,1024]{1,0:T(8,128)(2,1)} %bitcast.68, ...), custom_call_target="tpu_custom_call" | custom-call | bytes 131072 | tf_op jit(solution)/shard_map/outer_rows0/pallas_call | solution.py:429
  227.1 12.5 %outer_two0.1 = (bf16[128,5120]{1,0:T(8,128)(2,1)}, bf16[128,5120]{1,0:T(8,128)(2,1)}, bf16[128,5120]{1,0:T(8,128)(2,1)}, bf16[128,5120]{1,0:T(8,128)(2,1)}) custom-call(s32[5]{0:T(128)} %pad_add_fusion.scal, bf16[456,1024]{1,0:T(8,128)(2,1)} %get-tuple-element.189.x.refs_0_, bf16[456,1024]{1,0:T(8,128)(2,1)} %get-tuple-element.190.refs_1_, ...), custom_call_target="tpu_custom_call" | custom-call | bytes 163840 | tf_op jit(solution)/shard_map/outer_two0/pallas_call | solution.py:545
  243.1 25.8 %attend_back.1.refs_4_ = bf16[4,456,768]{2,1,0:T(8,128)(2,1)} custom-call(s32[5]{0:T(128)} %pad_add_fusion.scal, bf16[456,768]{1,0:T(8,128)(2,1)} %get-tuple-element.143.refs_0_.refs_4_.refs_8_, bf16[456,768]{1,0:T(8,128)(2,1)} %get-tuple-element.147.refs_1_.refs_5_.refs_9_, bf16[456,768]{1,0:T(8,128)(2,1)} %get-tuple-element.151.refs_2_.refs_6_.refs_10_, ...), custom_call_target="tpu_custom_call" | custom-call | bytes 134217728 | tf_op jit(solution)/shard_map/attend_back/pallas_call | solution.py:284
  273.5 4.8 %all-to-all-start.2 = ((bf16[4,456,768]{2,1,0:T(8,128)(2,1)}), bf16[4,456,768]{2,1,0:T(8,128)(2,1)}, u32[]{:S(2)}, u32[]{:S(2)}) async-start(bf16[4,456,768]{2,1,0:T(8,128)(2,1)} %attend_back.1.refs_4_), calls=%async_computation.2 | async-start | bytes 5603328 | tf_op jit(solution)/shard_map/all_to_all | solution.py:1023
  280.4 9.1 %outer_qkv1.1 = (bf16[4,128,768]{2,1,0:T(8,128)(2,1)}, f32[1,768]{1,0:T(1,128)}) custom-call(s32[5]{0:T(128)} %pad_add_fusion.scal, bf16[456,1024]{1,0:T(8,128)(2,1)} %get-tuple-element.214.refs_0_, bf16[456,1024]{1,0:T(8,128)(2,1)} %get-tuple-element.215.refs_1_, bf16[456,1024]{1,0:T(8,128)(2,1)} %get-tuple-element.216.refs_2_, ...), custom_call_target="tpu_custom_call" | custom-call | bytes 114432 | tf_op jit(solution)/shard_map/outer_qkv1/pallas_call | solution.py:483
  289.5 4.0 sides.4
  295.6 9.9 %narrow.1 = bf16[3,146,1024]{2,1,0:T(8,128)(2,1)} custom-call(s32[5]{0:T(128)} %pad_add_fusion.scal, bf16[456,4096]{1,0:T(8,128)(2,1)} %get-tuple-element.208.left.x, f32[456,1024]{1,0:T(8,128)} %get-tuple-element.178.refs_1_.mixed, f32[1,1024]{1,0:T(1,128)} %get-tuple-element.209.bias, bf16[4096,1024]{1,0:T(8,128)(2,1)} %all-gather.3.cloned.1.call-done.weight), custom_call_target="tpu_custom_call" | custom-call | bytes 233216 | tf_op jit(solution)/shard_map/narrow/pallas_call | solution.py:391
  309.9 4.8 %collective-permute-start.33 = (bf16[512,1024]{1,0:T(8,128)(2,1)}, bf16[512,1024]{1,0:T(8,128)(2,1)}, u32[]{:S(2)}, u32[]{:S(2)}) collective-permute-start(bf16[512,1024]{1,0:T(8,128)(2,1)} %total.9), channel_id=1, source_target_pairs={{0,1},{3,2},{4,5},{7,6},{8,9},{11,10},{12,13},{15,14},{16,17},{19,... | collective-permute-start | bytes 3145736 | tf_op jit(solution)/shard_map/ppermute | solution.py:951
  314.7 8.9 %outer_qkv0.1 = (bf16[128,768]{1,0:T(8,128)(2,1)}, bf16[128,768]{1,0:T(8,128)(2,1)}, bf16[128,768]{1,0:T(8,128)(2,1)}, bf16[128,768]{1,0:T(8,128)(2,1)}) custom-call(s32[5]{0:T(128)} %pad_add_fusion.scal, bf16[456,1024]{1,0:T(8,128)(2,1)} %get-tuple-element.214.refs_0_, bf16[456,1024]{1,0:T(8,128)(2,1)} %get-tuple-element.215.refs_1_, ...), custom_call_target="tpu_custom_call" | custom-call | bytes 126720 | tf_op jit(solution)/shard_map/outer_qkv0/pallas_call | solution.py:483
  323.6 7.3 %collective-permute-done.24.refs_1_ = bf16[128,5120]{1,0:T(8,128)(2,1)S(1)} collective-permute-done((bf16[128,5120]{1,0:T(8,128)(2,1)}, bf16[128,5120]{1,0:T(8,128)(2,1)S(1)}, u32[]{:S(2)}, u32[]{:S(2)}) %collective-permute-start.24) | collective-permute-done | bytes 1310752 | tf_op jit(solution)/shard_map/ppermute | solution.py:773
  343.1 11.6 %project_back.1 = (f32[3,146,1024]{2,1,0:T(8,128)}, f32[8,1024]{1,0:T(8,128)}) custom-call(s32[5]{0:T(128)} %pad_add_fusion.scal, bf16[4,456,768]{2,1,0:T(8,128)(2,1)} %all-to-all-done.2.refs_0_, bf16[456,1024]{1,0:T(8,128)(2,1)} %bitcast.71, f32[456,1024]{1,0:T(8,128)} %get-tuple-element.225.refs_2_, f32[1,1024]{1,0:T(1,128)} %get-tuple-element.139.refs_1_.refs_3_, ...), custom_call_target="tpu_custom_call" | custom-call | bytes 215040 | tf_op jit(solution)/shard_map/project_back/pallas_call | solution.py:746
  359.8 4.0 total.12.refs_0_
  365.4 7.0 %collective-permute-start.34 = (bf16[64,5120]{1,0:T(8,128)(2,1)S(1)}, bf16[64,5120]{1,0:T(8,128)(2,1)S(1)}, u32[]{:S(2)}, u32[]{:S(2)}) collective-permute-start(bf16[64,5120]{1,0:T(8,128)(2,1)S(1)} %copy-done.17), channel_id=1, source_target_pairs={{0,1},{3,2},{4,5},{7,6},{8,9},{11,10},{12,13},{15,14},{16,17},{19,... | collective-permute-start | bytes 1966088 | tf_op jit(solution)/shard_map/ppermute | solution.py:951
  408.8 26.0 %collective-permute-done.41.refs_1_ = bf16[512,1024]{1,0:T(8,128)(2,1)} collective-permute-done((bf16[512,1024]{1,0:T(8,128)(2,1)}, bf16[512,1024]{1,0:T(8,128)(2,1)}, u32[]{:S(2)}, u32[]{:S(2)}) %collective-permute-start.41) | collective-permute-done | bytes 1048608 | tf_op jit(solution)/shard_map/ppermute | solution.py:960
  451.0 13.9 %collective-permute-done.43.refs_3_ = bf16[64,5120]{1,0:T(8,128)(2,1)S(1)} collective-permute-done((bf16[64,5120]{1,0:T(8,128)(2,1)}, bf16[64,5120]{1,0:T(8,128)(2,1)S(1)}, u32[]{:S(2)}, u32[]{:S(2)}) %collective-permute-start.43) | collective-permute-done | bytes 655392 | tf_op jit(solution)/shard_map/ppermute | solution.py:960
  (195 shorter events, 134.6 us)
Async XLA Ops:
  7.2 129.1 %all-gather.3.cloned.1.call-start = ((), (), s32[]{:S(2)}) async-start(), calls=%async_computation.4 | async-start | bytes 9437184 | tf_op jit(solution)/shard_map/all_gather | solution.py:1073
  7.2 33.1 %collective-permute-start.2 = (bf16[3,146,1024]{2,1,0:T(8,128)(2,1)}, bf16[3,146,1024]{2,1,0:T(8,128)(2,1)}, u32[]{:S(2)}, u32[]{:S(2)}) collective-permute-start(bf16[3,146,1024]{2,1,0:T(8,128)(2,1)} %param.16), channel_id=1, source_target_pairs={{1,0},{2,1},{3,2},{5,4},{6,5},{7,6},{9,8},{10,9},{11,10},{13,12},{... | collective-permute-start | bytes 2691080 | tf_op jit(solution)/shard_map/ppermute | solution.py:1007
  8.5 31.8 %collective-permute-start = (bf16[3,146,1024]{2,1,0:T(8,128)(2,1)}, bf16[3,146,1024]{2,1,0:T(8,128)(2,1)}, u32[]{:S(2)}, u32[]{:S(2)}) collective-permute-start(bf16[3,146,1024]{2,1,0:T(8,128)(2,1)} %param.16), channel_id=1, source_target_pairs={{0,1},{1,2},{2,3},{4,5},{5,6},{6,7},{8,9},{9,10},{10,11},{12,13},{... | collective-permute-start | bytes 2691080 | tf_op jit(solution)/shard_map/ppermute | solution.py:1006
  17.8 21.2 %collective-permute-start.5 = (bf16[144,3072]{1,0:T(8,128)(2,1)S(1)}, bf16[144,3072]{1,0:T(8,128)(2,1)S(1)}, u32[]{:S(2)}, u32[]{:S(2)}) collective-permute-start(bf16[144,3072]{1,0:T(8,128)(2,1)S(1)} %fusion.2.refs_0_.refs_5_.refs_4_), channel_id=1, source_target_pairs={{0,16},{4,20},{8,24},{12,28},{16,0},{20,4},{24,8},{28,12},{1,17},{... | collective-permute-start | bytes 2654216 | tf_op jit(solution)/shard_map/ppermute | solution.py:773
  19.8 20.5 %collective-permute-start.4 = (bf16[144,3072]{1,0:T(8,128)(2,1)S(1)}, bf16[144,3072]{1,0:T(8,128)(2,1)S(1)}, u32[]{:S(2)}, u32[]{:S(2)}) collective-permute-start(bf16[144,3072]{1,0:T(8,128)(2,1)S(1)} %fusion.2.refs_0_.refs_5_.refs_4_), channel_id=1, source_target_pairs={{0,8},{4,12},{8,0},{12,4},{16,24},{20,28},{24,16},{28,20},{1,9},{5... | collective-permute-start | bytes 2654216 | tf_op jit(solution)/shard_map/ppermute | solution.py:773
  40.4 122.7 %all-gather.5.cloned.1.call-start = ((), (), s32[]{:S(2)}) async-start(), calls=%async_computation.5 | async-start | bytes 9437184 | tf_op jit(solution)/shard_map/all_gather | solution.py:1073
  41.2 27.4 %collective-permute-start.3 = (bf16[3,146,1024]{2,1,0:T(8,128)(2,1)}, bf16[3,146,1024]{2,1,0:T(8,128)(2,1)}, u32[]{:S(2)}, u32[]{:S(2)}) collective-permute-start(bf16[3,146,1024]{2,1,0:T(8,128)(2,1)} %collective-permute-done.2), channel_id=1, source_target_pairs={{1,0},{2,1},{5,4},{6,5},{9,8},{10,9},{13,12},{14,13},{17,16},{18,1... | collective-permute-start | bytes 2691080 | tf_op jit(solution)/shard_map/ppermute | solution.py:1007
  42.5 26.1 %collective-permute-start.1 = (bf16[3,146,1024]{2,1,0:T(8,128)(2,1)}, bf16[3,146,1024]{2,1,0:T(8,128)(2,1)}, u32[]{:S(2)}, u32[]{:S(2)}) collective-permute-start(bf16[3,146,1024]{2,1,0:T(8,128)(2,1)} %collective-permute-done), channel_id=1, source_target_pairs={{1,2},{2,3},{5,6},{6,7},{9,10},{10,11},{13,14},{14,15},{17,18},{18... | collective-permute-start | bytes 2691080 | tf_op jit(solution)/shard_map/ppermute | solution.py:1006
  44.1 24.4 %collective-permute-start.9 = (bf16[144,3072]{1,0:T(8,128)(2,1)S(1)}, bf16[144,3072]{1,0:T(8,128)(2,1)}, u32[]{:S(2)}, u32[]{:S(2)}) collective-permute-start(bf16[144,3072]{1,0:T(8,128)(2,1)S(1)} %broadcast_select_fusion), channel_id=1, source_target_pairs={{0,8},{4,20},{8,0},{12,28},{16,24},{20,4},{24,16},{28,12},{1,9},{5... | collective-permute-start | bytes 2654216 | tf_op jit(solution)/shard_map/ppermute | solution.py:777
  45.7 27.1 %collective-permute-start.6 = (bf16[144,3072]{1,0:T(8,128)(2,1)S(1)}, bf16[144,3072]{1,0:T(8,128)(2,1)}, u32[]{:S(2)}, u32[]{:S(2)}) collective-permute-start(bf16[144,3072]{1,0:T(8,128)(2,1)S(1)} %fusion.2.refs_0_.refs_5_.refs_4_), channel_id=1, source_target_pairs={{0,4},{4,0},{8,12},{12,8},{16,20},{20,16},{24,28},{28,24},{1,5},{5... | collective-permute-start | bytes 2654216 | tf_op jit(solution)/shard_map/ppermute | solution.py:773
  71.5 32.1 %collective-permute-start.12 = (bf16[3,146,1024]{2,1,0:T(8,128)(2,1)}, bf16[3,146,1024]{2,1,0:T(8,128)(2,1)}, u32[]{:S(2)}, u32[]{:S(2)}) collective-permute-start(bf16[3,146,1024]{2,1,0:T(8,128)(2,1)} %collective-permute-done.3), channel_id=1, source_target_pairs={{1,0},{5,4},{9,8},{13,12},{17,16},{21,20},{25,24},{29,28}} | collective-permute-start | bytes 2691080 | tf_op jit(solution)/shard_map/ppermute | solution.py:1007
  72.8 30.9 %collective-permute-start.11 = (bf16[3,146,1024]{2,1,0:T(8,128)(2,1)}, bf16[3,146,1024]{2,1,0:T(8,128)(2,1)}, u32[]{:S(2)}, u32[]{:S(2)}) collective-permute-start(bf16[3,146,1024]{2,1,0:T(8,128)(2,1)} %collective-permute-done.1), channel_id=1, source_target_pairs={{2,3},{6,7},{10,11},{14,15},{18,19},{22,23},{26,27},{30,31}} | collective-permute-start | bytes 2691080 | tf_op jit(solution)/shard_map/ppermute | solution.py:1006
  101.2 24.8 %collective-permute-start.15 = (bf16[128,1024]{1,0:T(8,128)(2,1)S(1)}, bf16[128,1024]{1,0:T(8,128)(2,1)S(1)}, u32[]{:S(2)}, u32[]{:S(2)}) collective-permute-start(bf16[128,1024]{1,0:T(8,128)(2,1)S(1)} %copy-done.10), channel_id=1, source_target_pairs={{0,4},{4,0},{8,12},{12,8},{16,20},{20,16},{24,28},{28,24},{1,5},{5... | collective-permute-start | bytes 786440 | tf_op jit(solution)/shard_map/ppermute | solution.py:773
  101.6 24.4 %collective-permute-start.14 = (bf16[128,1024]{1,0:T(8,128)(2,1)S(1)}, bf16[128,1024]{1,0:T(8,128)(2,1)S(1)}, u32[]{:S(2)}, u32[]{:S(2)}) collective-permute-start(bf16[128,1024]{1,0:T(8,128)(2,1)S(1)} %copy-done.10), channel_id=1, source_target_pairs={{0,16},{4,20},{8,24},{12,28},{16,0},{20,4},{24,8},{28,12},{1,17},{... | collective-permute-start | bytes 786440 | tf_op jit(solution)/shard_map/ppermute | solution.py:773
  102.0 24.1 %collective-permute-start.13 = (bf16[128,1024]{1,0:T(8,128)(2,1)S(1)}, bf16[128,1024]{1,0:T(8,128)(2,1)S(1)}, u32[]{:S(2)}, u32[]{:S(2)}) collective-permute-start(bf16[128,1024]{1,0:T(8,128)(2,1)S(1)} %copy-done.10), channel_id=1, source_target_pairs={{0,8},{4,12},{8,0},{12,4},{16,24},{20,28},{24,16},{28,20},{1,9},{5... | collective-permute-start | bytes 786440 | tf_op jit(solution)/shard_map/ppermute | solution.py:773
  126.0 29.6 %all-to-all-start = ((bf16[4,456,256]{2,1,0:T(8,128)(2,1)}), bf16[4,456,256]{2,1,0:T(8,128)(2,1)S(1)}, u32[]{:S(2)}, u32[]{:S(2)}) async-start(bf16[4,456,256]{2,1,0:T(8,128)(2,1)} %get-tuple-element.160), calls=%async_computation | async-start | bytes 1867776 | tf_op jit(solution)/shard_map/all_to_all | solution.py:1023
  214.9 27.2 %all-to-all-start.1 = ((bf16[4,456,256]{2,1,0:T(8,128)(2,1)}), bf16[4,456,256]{2,1,0:T(8,128)(2,1)S(1)}, u32[]{:S(2)}, u32[]{:S(2)}) async-start(bf16[4,456,256]{2,1,0:T(8,128)(2,1)} %mix_back.1), calls=%async_computation.1 | async-start | bytes 1867776 | tf_op jit(solution)/shard_map/all_to_all | solution.py:1023
  239.6 34.0 %collective-permute-start.22 = (bf16[128,5120]{1,0:T(8,128)(2,1)}, bf16[128,5120]{1,0:T(8,128)(2,1)}, u32[]{:S(2)}, u32[]{:S(2)}) collective-permute-start(bf16[128,5120]{1,0:T(8,128)(2,1)} %get-tuple-element.193), channel_id=1, source_target_pairs={{0,8},{4,20},{8,0},{12,28},{16,24},{20,4},{24,16},{28,12},{1,9},{5... | collective-permute-start | bytes 3932168 | tf_op jit(solution)/shard_map/ppermute | solution.py:777
  241.2 27.7 %collective-permute-start.23 = (bf16[512,1024]{1,0:T(8,128)(2,1)}, bf16[512,1024]{1,0:T(8,128)(2,1)S(1)}, u32[]{:S(2)}, u32[]{:S(2)}) collective-permute-start(bf16[512,1024]{1,0:T(8,128)(2,1)} %get-tuple-element.188), channel_id=1, source_target_pairs={{0,8},{4,20},{8,0},{12,28},{16,24},{20,4},{24,16},{28,12},{1,9},{5... | collective-permute-start | bytes 3145736 | tf_op jit(solution)/shard_map/ppermute | solution.py:777
  273.5 69.6 %all-to-all-start.2 = ((bf16[4,456,768]{2,1,0:T(8,128)(2,1)}), bf16[4,456,768]{2,1,0:T(8,128)(2,1)}, u32[]{:S(2)}, u32[]{:S(2)}) async-start(bf16[4,456,768]{2,1,0:T(8,128)(2,1)} %attend_back.1.refs_4_), calls=%async_computation.2 | async-start | bytes 5603328 | tf_op jit(solution)/shard_map/all_to_all | solution.py:1023
  278.4 27.1 %collective-permute-start.26 = (bf16[512,1024]{1,0:T(8,128)(2,1)}, bf16[512,1024]{1,0:T(8,128)(2,1)}, u32[]{:S(2)}, u32[]{:S(2)}) collective-permute-start(bf16[512,1024]{1,0:T(8,128)(2,1)} %get-tuple-element.201), channel_id=1, source_target_pairs={{0,8},{4,12},{8,0},{12,4},{16,24},{20,28},{24,16},{28,20},{1,9},{5... | collective-permute-start | bytes 3145736 | tf_op jit(solution)/shard_map/ppermute | solution.py:773
  280.1 26.3 %collective-permute-start.27 = (bf16[512,1024]{1,0:T(8,128)(2,1)}, bf16[512,1024]{1,0:T(8,128)(2,1)}, u32[]{:S(2)}, u32[]{:S(2)}) collective-permute-start(bf16[512,1024]{1,0:T(8,128)(2,1)} %get-tuple-element.202), channel_id=1, source_target_pairs={{0,16},{4,20},{8,24},{12,28},{16,0},{20,4},{24,8},{28,12},{1,17},{... | collective-permute-start | bytes 3145736 | tf_op jit(solution)/shard_map/ppermute | solution.py:773
  293.5 37.4 %collective-permute-start.24 = (bf16[128,5120]{1,0:T(8,128)(2,1)}, bf16[128,5120]{1,0:T(8,128)(2,1)S(1)}, u32[]{:S(2)}, u32[]{:S(2)}) collective-permute-start(bf16[128,5120]{1,0:T(8,128)(2,1)} %get-tuple-element.206), channel_id=1, source_target_pairs={{0,8},{4,12},{8,0},{12,4},{16,24},{20,28},{24,16},{28,20},{1,9},{5... | collective-permute-start | bytes 3932168 | tf_op jit(solution)/shard_map/ppermute | solution.py:773
  294.8 37.6 %collective-permute-start.25 = (bf16[128,5120]{1,0:T(8,128)(2,1)}, bf16[128,5120]{1,0:T(8,128)(2,1)}, u32[]{:S(2)}, u32[]{:S(2)}) collective-permute-start(bf16[128,5120]{1,0:T(8,128)(2,1)} %get-tuple-element.207), channel_id=1, source_target_pairs={{0,16},{4,20},{8,24},{12,28},{16,0},{20,4},{24,8},{28,12},{1,17},{... | collective-permute-start | bytes 3932168 | tf_op jit(solution)/shard_map/ppermute | solution.py:773
  309.9 48.1 %collective-permute-start.33 = (bf16[512,1024]{1,0:T(8,128)(2,1)}, bf16[512,1024]{1,0:T(8,128)(2,1)}, u32[]{:S(2)}, u32[]{:S(2)}) collective-permute-start(bf16[512,1024]{1,0:T(8,128)(2,1)} %total.9), channel_id=1, source_target_pairs={{0,1},{3,2},{4,5},{7,6},{8,9},{11,10},{12,13},{15,14},{16,17},{19,... | collective-permute-start | bytes 3145736 | tf_op jit(solution)/shard_map/ppermute | solution.py:951
  335.5 24.3 %collective-permute-start.32 = (bf16[64,5120]{1,0:T(8,128)(2,1)}, bf16[64,5120]{1,0:T(8,128)(2,1)S(1)}, u32[]{:S(2)}, u32[]{:S(2)}) collective-permute-start(bf16[64,5120]{1,0:T(8,128)(2,1)} %total.10), channel_id=1, source_target_pairs={{0,1},{3,2},{4,5},{7,6},{8,9},{11,10},{12,13},{15,14},{16,17},{19,... | collective-permute-start | bytes 1966088 | tf_op jit(solution)/shard_map/ppermute | solution.py:951
  363.8 33.4 %collective-permute-start.39 = (bf16[512,1024]{1,0:T(8,128)(2,1)}, bf16[512,1024]{1,0:T(8,128)(2,1)}, u32[]{:S(2)}, u32[]{:S(2)}) collective-permute-start(bf16[512,1024]{1,0:T(8,128)(2,1)} %total.12.refs_0_), channel_id=1, source_target_pairs={{1,2},{2,1},{5,6},{6,5},{9,10},{10,9},{13,14},{14,13},{17,18},{18,... | collective-permute-start | bytes 3145736 | tf_op jit(solution)/shard_map/ppermute | solution.py:955
  393.7 48.9 %all-to-all-start.3 = ((bf16[4,144,768]{2,1,0:T(8,128)(2,1)}), bf16[4,144,768]{2,1,0:T(8,128)(2,1)S(1)}, u32[]{:S(2)}, u32[]{:S(2)}) async-start(bf16[4,144,768]{2,1,0:T(8,128)(2,1)} %copies.1), calls=%async_computation.3 | async-start | bytes 1769472 | tf_op jit(solution)/shard_map/all_to_all | solution.py:1023
  400.5 34.3 %collective-permute-start.41 = (bf16[512,1024]{1,0:T(8,128)(2,1)}, bf16[512,1024]{1,0:T(8,128)(2,1)}, u32[]{:S(2)}, u32[]{:S(2)}) collective-permute-start(bf16[512,1024]{1,0:T(8,128)(2,1)} %total.15.refs_0_), channel_id=1, source_target_pairs={{1,0},{2,3},{5,4},{6,7},{9,8},{10,11},{13,12},{14,15},{17,16},{18,... | collective-permute-start | bytes 3145736 | tf_op jit(solution)/shard_map/ppermute | solution.py:960
  403.3 35.3 %collective-permute-start.40 = (bf16[64,5120]{1,0:T(8,128)(2,1)S(1)}, bf16[64,5120]{1,0:T(8,128)(2,1)}, u32[]{:S(2)}, u32[]{:S(2)}) collective-permute-start(bf16[64,5120]{1,0:T(8,128)(2,1)S(1)} %copy-done.7), channel_id=1, source_target_pairs={{1,2},{2,1},{5,6},{6,5},{9,10},{10,9},{13,14},{14,13},{17,18},{18,... | collective-permute-start | bytes 1966088 | tf_op jit(solution)/shard_map/ppermute | solution.py:955
  407.5 43.5 %collective-permute-start.42 = (bf16[64,5120]{1,0:T(8,128)(2,1)}, bf16[64,5120]{1,0:T(8,128)(2,1)}, u32[]{:S(2)}, u32[]{:S(2)}) collective-permute-start(bf16[64,5120]{1,0:T(8,128)(2,1)} %total.16.refs_0_), channel_id=1, source_target_pairs={{1,0},{2,3},{5,4},{6,7},{9,8},{10,11},{13,12},{14,15},{17,16},{18,... | collective-permute-start | bytes 1966088 | tf_op jit(solution)/shard_map/ppermute | solution.py:960
  441.3 23.6 %collective-permute-start.43 = (bf16[64,5120]{1,0:T(8,128)(2,1)}, bf16[64,5120]{1,0:T(8,128)(2,1)S(1)}, u32[]{:S(2)}, u32[]{:S(2)}) collective-permute-start(bf16[64,5120]{1,0:T(8,128)(2,1)} %total.17.refs_1_), channel_id=1, source_target_pairs={{1,0},{2,3},{5,4},{6,7},{9,8},{10,11},{13,12},{14,15},{17,16},{18,... | collective-permute-start | bytes 1966088 | tf_op jit(solution)/shard_map/ppermute | solution.py:960
  (48 other events, 457.8 us)
Sparse Core Ops, SparseCore 0:
  40.5 58.3 all-gather.2
  100.8 57.7 all-gather.4
